TPU v7x, 128 devices: a whole 4x4x4 slice. The times are simulated.
128 devices in a mesh: gx: 8 (over x, z_hi), gy: 16 (over z_lo, y, core).
Axes of the slice: x: 4, y: 4, z: 4 (z_hi: 2, z_lo: 2; z = z_hi * 2 + z_lo), core: 2. Of those that a mesh axis runs over, the one named last changes fastest.
Arguments:
- flow_state: float32 [4, 2048, 4096], P(None, 'gx', 'gy'), may hold values from -0.4 to 3.5, as said below
- cell_kind: int32 [2048, 4096], P('gx', 'gy'), may hold values from 0 to 2
Outputs:
- new_state: float32 [4, 2048, 4096], P(None, 'gx', 'gy')
- fine_residual: float32 [4, 2048, 4096], P(None, 'gx', 'gy')
Inputs may be any that keep to these rules, and one draw needn't show every extreme that they name: `flow_state`: every cell holds the conserved variables of a state with density 0.8 to 1.25, velocity components -0.3 to 0.3 and pressure 0.7 to 1.3.
All inputs are finite; a program needn't handle non-finite values.
Results may differ from a plain program's by a relative error of at most 0.00002.
Values sent between devices are 32-bit elements; how exact they have to be, the bound alone decides.
A program may use at most 64 MiB of HBM per device.

v0:
```python
import jax
import jax.numpy as jnp
from jax import lax
from jax.sharding import PartitionSpec as P

courant = 0.4
kappa_two = 0.25
kappa_four = 1.0 / 32.0


def with_halo(value, sides, width):
    for axis, dim in sides:
        count, length = (lax.axis_size(axis), value.shape[dim])
        up = [(i, (i + 1) % count) for i in range(count)]
        down = [(j, i) for i, j in up]
        last = lax.slice_in_dim(value, length - width, length, axis=dim)
        first = lax.slice_in_dim(value, 0, width, axis=dim)
        before = lax.ppermute(last, axis, up)
        after = lax.ppermute(first, axis, down)
        value = jnp.concatenate([before, value, after], axis=dim)
    return value


def swapped(block, axis, stride):
    count = lax.axis_size(axis)
    route = []
    for low in range(count):
        high = low | 1 << stride
        if high != low and high < count:
            route += [(low, high), (high, low)]
    return lax.ppermute(block, axis, route)


def section(field, start, stop, axis_dim):
    return lax.slice_in_dim(field, start, stop, axis=axis_dim)


def sweep(strip_cells, normal, axis_dim):
    length = strip_cells.shape[axis_dim] - 4
    density = strip_cells[0:1]
    momentum_x = strip_cells[1:2]
    momentum_y = strip_cells[2:3]
    energy = strip_cells[3:4]
    inverse = 1.0 / density
    speed_x = momentum_x * inverse
    speed_y = momentum_y * inverse
    pressure = 0.4 * (energy - 0.5 * (momentum_x * speed_x + momentum_y * speed_y))
    if normal == 1:
        normal_speed = speed_x
        flux = jnp.concatenate(
            [
                momentum_x,
                momentum_x * speed_x + pressure,
                momentum_y * speed_x,
                (energy + pressure) * speed_x,
            ],
            0,
        )
    else:
        normal_speed = speed_y
        flux = jnp.concatenate(
            [
                momentum_y,
                momentum_x * speed_y,
                momentum_y * speed_y + pressure,
                (energy + pressure) * speed_y,
            ],
            0,
        )
    spectral = jnp.abs(normal_speed) + jnp.sqrt(1.4 * pressure * inverse)
    press_low = section(pressure, 0, length + 2, axis_dim)
    press_mid = section(pressure, 1, length + 3, axis_dim)
    press_high = section(pressure, 2, length + 4, axis_dim)
    sensor = jnp.abs(press_high - 2.0 * press_mid + press_low) / (
        press_high + 2.0 * press_mid + press_low
    )
    second_coef = kappa_two * jnp.maximum(
        section(sensor, 0, length + 1, axis_dim), section(sensor, 1, length + 2, axis_dim)
    )
    fourth_coef = jnp.maximum(0.0, kappa_four - second_coef)
    cell_back = section(strip_cells, 0, length + 1, axis_dim)
    cell_left = section(strip_cells, 1, length + 2, axis_dim)
    cell_right = section(strip_cells, 2, length + 3, axis_dim)
    cell_ahead = section(strip_cells, 3, length + 4, axis_dim)
    face_spectral = 0.5 * (
        section(spectral, 1, length + 2, axis_dim) + section(spectral, 2, length + 3, axis_dim)
    )
    central = 0.5 * (
        section(flux, 1, length + 2, axis_dim) + section(flux, 2, length + 3, axis_dim)
    )
    damping = second_coef * (cell_right - cell_left) - fourth_coef * (
        cell_ahead - 3.0 * cell_right + 3.0 * cell_left - cell_back
    )
    face_flux = central - face_spectral * damping
    divergence = section(face_flux, 1, length + 1, axis_dim) - section(
        face_flux, 0, length, axis_dim
    )
    return (divergence, section(spectral, 2, length + 2, axis_dim))


def residual(strip_x, strip_y, wall_share, far_share, spacing):
    div_x, spec_x = sweep(strip_x, 1, 1)
    div_y, spec_y = sweep(strip_y, 2, 2)
    cells = strip_x[:, 2:-2, :]
    free_stream = jnp.array([1.0, 0.5, 0.0, 1.0 / 0.56 + 0.125], dtype=jnp.float32).reshape(4, 1, 1)
    momentum_rate = jnp.array([0.0, 2.0, 2.0, 0.0], dtype=jnp.float32).reshape(4, 1, 1)
    source = wall_share[None] * momentum_rate * cells + far_share[None] * (cells - free_stream)
    return (spacing * (div_x + div_y) + spacing * spacing * source, spec_x + spec_y)


def coarse(field):
    return field[:, 0::2, 0::2] + field[:, 1::2, 0::2] + field[:, 0::2, 1::2] + field[:, 1::2, 1::2]


def cell_rims(field):
    return with_halo(field, (("gx", 1), ("gy", 2)), 2)


def pair_x(field):
    return swapped(field, "gx", 0)


def pair_y(field):
    return swapped(field, "gy", 0)


def join_pair(mine, partner, is_even, axis_dim):
    lower = jnp.where(is_even, mine, partner)
    higher = jnp.where(is_even, partner, mine)
    return jnp.concatenate([lower, higher], axis_dim)


def coarse_smooth(coarse_state, coarse_sum, coarse_wall, coarse_far, make_strips):
    strip_x, strip_y = make_strips(coarse_state)
    coarse_start, coarse_spectral = residual(strip_x, strip_y, coarse_wall, coarse_far, 2.0)
    forcing = coarse_sum - coarse_start
    coarse_segment = coarse_state - courant / coarse_spectral * coarse_sum * 0.5
    strip_x, strip_y = make_strips(coarse_segment)
    segment_residual, unused_more = residual(strip_x, strip_y, coarse_wall, coarse_far, 2.0)
    coarse_final = coarse_state - courant / coarse_spectral * (segment_residual + forcing) * 0.5
    return coarse_final - coarse_state


def local(flow_state, cell_kind):
    wall_share = (cell_kind == 1).astype(jnp.float32)
    far_share = (cell_kind == 2).astype(jnp.float32)
    even_x = lax.axis_index("gx") % 2 == 0
    even_y = lax.axis_index("gy") % 2 == 0

    def fine_strips(field):
        padded = cell_rims(field)
        return (padded[:, :, 2:-2], padded[:, 2:-2, :])

    strip_x, strip_y = fine_strips(flow_state)
    start_residual, start_spectral = residual(strip_x, strip_y, wall_share, far_share, 1.0)
    smoothed = flow_state - courant / start_spectral * start_residual
    strip_x, strip_y = fine_strips(smoothed)
    fine_residual, unused_spec = residual(strip_x, strip_y, wall_share, far_share, 1.0)
    quarter = jnp.concatenate(
        [
            0.25 * coarse(smoothed),
            coarse(fine_residual),
            0.25 * coarse(wall_share[None]),
            0.25 * coarse(far_share[None]),
        ],
        0,
    )
    halfway = join_pair(quarter, pair_x(quarter), even_x, 1)
    coarse_block = join_pair(halfway, pair_y(halfway), even_y, 2)

    def coarse_strips(field):
        padded = cell_rims(field)
        near_low_x = padded[:, :2, 2:-2]
        near_high_x = padded[:, -2:, 2:-2]
        partner_x = pair_x(jnp.where(even_x, near_low_x, near_high_x))
        low_x = jnp.where(even_x, near_low_x, partner_x)
        high_x = jnp.where(even_x, partner_x, near_high_x)
        near_low_y = padded[:, 2:-2, :2]
        near_high_y = padded[:, 2:-2, -2:]
        partner_y = pair_y(jnp.where(even_y, near_low_y, near_high_y))
        low_y = jnp.where(even_y, near_low_y, partner_y)
        high_y = jnp.where(even_y, partner_y, near_high_y)
        return (
            jnp.concatenate([low_x, field, high_x], 1),
            jnp.concatenate([low_y, field, high_y], 2),
        )

    correction = coarse_smooth(
        coarse_block[0:4], coarse_block[4:8], coarse_block[8], coarse_block[9], coarse_strips
    )
    half_rows = flow_state.shape[1] // 2
    half_cols = flow_state.shape[2] // 2
    start_x = lax.axis_index("gx") % 2 * half_rows
    start_y = lax.axis_index("gy") % 2 * half_cols
    zero_start = jnp.zeros((), jnp.int32)
    my_part = lax.dynamic_slice(
        correction, (zero_start, start_x, start_y), (4, half_rows, half_cols)
    )
    doubled_rows = jnp.repeat(my_part, 2, axis=1)
    new_state = smoothed.at[:, :, 0::2].add(doubled_rows).at[:, :, 1::2].add(doubled_rows)
    return (new_state, fine_residual)


def solution(mesh):
    return jax.shard_map(
        local,
        mesh=mesh,
        in_specs=(P(None, "gx", "gy"), P("gx", "gy")),
        out_specs=(P(None, "gx", "gy"), P(None, "gx", "gy")),
        check_vma=False,
    )
```

profile of v0, /device:TPU:0, one launch (start us, length us, event | category | flops | bytes accessed | tf_op | source)
XLA Modules:
  0.0 747.4 jit_solution(5465994704193269774)
XLA Ops:
  1.4 4.1 collective-permute-start
  9.0 28.3 %slice.734 = f32[1,128,128]{2,0,1:T(1,128)S(1)} slice(f32[1,256,256]{2,0,1:T(1,128)S(1)} %broadcast_in_dim.6), slice={[0:1:1], [0:256:2], [0:256:2]} | slice | bytes 131072 | tf_op jit(solution)/shard_map/slice | solution.py:112
  37.3 29.7 %slice.735 = f32[1,128,128]{2,0,1:T(1,128)S(1)} slice(f32[1,256,256]{2,0,1:T(1,128)S(1)} %broadcast_in_dim.6), slice={[0:1:1], [1:256:2], [0:256:2]} | slice | bytes 131072 | tf_op jit(solution)/shard_map/slice | solution.py:112
  67.0 28.3 %slice.736 = f32[1,128,128]{2,0,1:T(1,128)S(1)} slice(f32[1,256,256]{2,0,1:T(1,128)S(1)} %broadcast_in_dim.6), slice={[0:1:1], [0:256:2], [1:256:2]} | slice | bytes 131072 | tf_op jit(solution)/shard_map/slice | solution.py:112
  95.3 29.7 %slice.737 = f32[1,128,128]{2,0,1:T(1,128)S(1)} slice(f32[1,256,256]{2,0,1:T(1,128)S(1)} %broadcast_in_dim.6), slice={[0:1:1], [1:256:2], [1:256:2]} | slice | bytes 131072 | tf_op jit(solution)/shard_map/slice | solution.py:112
  125.2 28.3 %slice.738 = f32[1,128,128]{2,0,1:T(1,128)S(1)} slice(f32[1,256,256]{2,0,1:T(1,128)S(1)} %broadcast_in_dim.7), slice={[0:1:1], [0:256:2], [0:256:2]} | slice | bytes 131072 | tf_op jit(solution)/shard_map/slice | solution.py:112
  153.5 29.7 %slice.739 = f32[1,128,128]{2,0,1:T(1,128)S(1)} slice(f32[1,256,256]{2,0,1:T(1,128)S(1)} %broadcast_in_dim.7), slice={[0:1:1], [1:256:2], [0:256:2]} | slice | bytes 131072 | tf_op jit(solution)/shard_map/slice | solution.py:112
  183.2 28.3 %slice.740 = f32[1,128,128]{2,0,1:T(1,128)S(1)} slice(f32[1,256,256]{2,0,1:T(1,128)S(1)} %broadcast_in_dim.7), slice={[0:1:1], [0:256:2], [1:256:2]} | slice | bytes 131072 | tf_op jit(solution)/shard_map/slice | solution.py:112
  211.6 29.7 %slice.741 = f32[1,128,128]{2,0,1:T(1,128)S(1)} slice(f32[1,256,256]{2,0,1:T(1,128)S(1)} %broadcast_in_dim.7), slice={[0:1:1], [1:256:2], [1:256:2]} | slice | bytes 131072 | tf_op jit(solution)/shard_map/slice | solution.py:112
  255.9 3.9 collective-permute-start.3
  266.2 6.0 sqrt_add_fusion.3
  280.3 5.7 fusion.28
  288.6 28.3 %slice.684 = f32[4,128,128]{2,0,1:T(4,128)S(1)} slice(f32[4,256,256]{2,0,1:T(4,128)S(1)} %fusion.71), slice={[0:4:1], [0:256:2], [0:256:2]} | slice | bytes 524288 | tf_op jit(solution)/shard_map/slice | solution.py:112
  317.0 29.7 %slice.685 = f32[4,128,128]{2,0,1:T(4,128)S(1)} slice(f32[4,256,256]{2,0,1:T(4,128)S(1)} %fusion.71), slice={[0:4:1], [1:256:2], [0:256:2]} | slice | bytes 524288 | tf_op jit(solution)/shard_map/slice | solution.py:112
  346.7 28.3 %slice.686 = f32[4,128,128]{2,0,1:T(4,128)S(1)} slice(f32[4,256,256]{2,0,1:T(4,128)S(1)} %fusion.71), slice={[0:4:1], [0:256:2], [1:256:2]} | slice | bytes 524288 | tf_op jit(solution)/shard_map/slice | solution.py:112
  375.0 29.7 %slice.687 = f32[4,128,128]{2,0,1:T(4,128)S(1)} slice(f32[4,256,256]{2,0,1:T(4,128)S(1)} %fusion.71), slice={[0:4:1], [1:256:2], [1:256:2]} | slice | bytes 524288 | tf_op jit(solution)/shard_map/slice | solution.py:112
  406.0 4.4 collective-permute-start.5
  421.4 3.8 collective-permute-start.7
  430.5 9.9 %sqrt_add_fusion.2 = (f32[1,256,260]{2,0,1:T(1,128)S(1)}, f32[1,256,260]{2,0,1:T(1,128)S(1)}, f32[1,256,260]{2,0,1:T(1,128)S(1)}, f32[1,256,260]{2,0,1:T(1,128)S...) fusion(f32[4,260,2]{2,0,1:T(4,128)} %copy.195, f32[4,2,256]{2,0,1:T(4,128)S(1)} %collective-permute-done.5, ...), kind=kLoop, calls=%fused_computation.254 | loop fusion | flops 1863680 | bytes 2679040 | tf_op jit(solution)/shard_map/add | solution.py:70
  450.7 3.7 fusion.21
  455.3 28.3 %slice.732 = f32[4,128,128]{2,0,1:T(4,128)S(1)} slice(f32[4,256,256]{2,0,1:T(4,128)S(1)} %fusion.73), slice={[0:4:1], [0:256:2], [1:256:2]} | slice | bytes 524288 | tf_op jit(solution)/shard_map/slice | solution.py:112
  483.6 28.3 %slice.730 = f32[4,128,128]{2,0,1:T(4,128)S(1)} slice(f32[4,256,256]{2,0,1:T(4,128)S(1)} %fusion.73), slice={[0:4:1], [0:256:2], [0:256:2]} | slice | bytes 524288 | tf_op jit(solution)/shard_map/slice | solution.py:112
  511.9 29.7 %slice.731 = f32[4,128,128]{2,0,1:T(4,128)S(1)} slice(f32[4,256,256]{2,0,1:T(4,128)S(1)} %fusion.73), slice={[0:4:1], [1:256:2], [0:256:2]} | slice | bytes 524288 | tf_op jit(solution)/shard_map/slice | solution.py:112
  541.6 50.9 %slice.733 = f32[4,128,128]{2,0,1:T(4,128)} slice(f32[4,256,256]{2,0,1:T(4,128)S(1)} %fusion.73), slice={[0:4:1], [1:256:2], [1:256:2]} | slice | bytes 524288 | tf_op jit(solution)/shard_map/slice | solution.py:112
  596.5 13.3 %collective-permute-done.8 = f32[10,128,128]{2,1,0:T(8,128)S(1)} collective-permute-done((f32[10,128,128]{2,1,0:T(8,128)S(1)}, f32[10,128,128]{2,1,0:T(8,128)S(1)}, u32[]{:S(2)}, u32[]{:S(2)}) %collective-permute-start.8) | collective-permute-done | bytes 655392 | tf_op jit(solution)/shard_map/ppermute | solution.py:31
  619.9 4.2 collective-permute-start.11
  643.0 3.9 collective-permute-start.14
  671.1 5.5 fusion.6
  701.7 3.9 collective-permute-start.20
  727.7 5.3 fusion.14
  735.5 5.1 scatter_fusion
  740.7 5.1 scatter_fusion.1
  (285 shorter events, 172.0 us)
Async XLA Ops:
  1.4 240.7 %collective-permute-start = (f32[4,2,256]{2,0,1:T(4,128)S(1)}, f32[4,2,256]{2,0,1:T(4,128)S(1)}, u32[]{:S(2)}, u32[]{:S(2)}) collective-permute-start(f32[4,2,256]{2,0,1:T(4,128)S(1)} %copy.304), channel_id=1, source_target_pairs={{0,16},{16,32},{32,48},{48,64},{64,80},{80,96},{96,112},{112,0},{1... | collective-permute-start | bytes 24584 | tf_op jit(solution)/shard_map/ppermute | solution.py:18
  5.5 237.8 %collective-permute-start.1 = (f32[4,2,256]{2,0,1:T(4,128)S(1)}, f32[4,2,256]{2,0,1:T(4,128)S(1)}, u32[]{:S(2)}, u32[]{:S(2)}) collective-permute-start(f32[4,2,256]{2,0,1:T(4,128)S(1)} %copy.305), channel_id=1, source_target_pairs={{16,0},{32,16},{48,32},{64,48},{80,64},{96,80},{112,96},{0,112},{1... | collective-permute-start | bytes 24584 | tf_op jit(solution)/shard_map/ppermute | solution.py:19
  8.8 233.4 %copy-start.19 = (f32[256,256]{1,0:T(8,128)}, f32[256,256]{1,0:T(8,128)S(1)}, u32[]{:S(2)}) copy-start(f32[256,256]{1,0:T(8,128)S(1)} %get-tuple-element.138) | copy-start | bytes 786436
  8.8 233.4 %copy-start.15 = (f32[4,256,256]{2,1,0:T(8,128)S(1)}, f32[4,256,256]{2,1,0:T(8,128)}, u32[]{:S(2)}) copy-start(f32[4,256,256]{2,1,0:T(8,128)} %param.10) | copy-start | bytes 3145732
  252.5 8.4 %copy-start.32 = (f32[1,260,256]{2,0,1:T(1,128)S(1)}, f32[1,260,256]{2,0,1:T(1,128)}, u32[]{:S(2)}) copy-start(f32[1,260,256]{2,0,1:T(1,128)} %get-tuple-element.81) | copy-start | bytes 798724
  252.5 8.4 %copy-start.33 = (f32[1,260,256]{2,0,1:T(1,128)S(1)}, f32[1,260,256]{2,0,1:T(1,128)}, u32[]{:S(2)}) copy-start(f32[1,260,256]{2,0,1:T(1,128)} %get-tuple-element.82) | copy-start | bytes 798724
  252.5 8.4 %copy-start.34 = (f32[1,260,256]{2,0,1:T(1,128)S(1)}, f32[1,260,256]{2,0,1:T(1,128)}, u32[]{:S(2)}) copy-start(f32[1,260,256]{2,0,1:T(1,128)} %get-tuple-element.89) | copy-start | bytes 798724
  254.5 10.2 %collective-permute-start.2 = (f32[4,260,2]{1,0,2:T(4,128)S(1)}, f32[4,260,2]{1,0,2:T(4,128)S(1)}, u32[]{:S(2)}, u32[]{:S(2)}) collective-permute-start(f32[4,260,2]{1,0,2:T(4,128)S(1)} %copy.175), channel_id=1, source_target_pairs={{0,1},{1,2},{2,3},{3,4},{4,5},{5,6},{6,7},{7,8},{8,9},{9,10},{10,1... | collective-permute-start | bytes 24968 | tf_op jit(solution)/shard_map/ppermute | solution.py:18
  255.9 9.2 %collective-permute-start.3 = (f32[4,260,2]{1,0,2:T(4,128)S(1)}, f32[4,260,2]{1,0,2:T(4,128)}, u32[]{:S(2)}, u32[]{:S(2)}) collective-permute-start(f32[4,260,2]{1,0,2:T(4,128)S(1)} %copy.176), channel_id=1, source_target_pairs={{1,0},{2,1},{3,2},{4,3},{5,4},{6,5},{7,6},{8,7},{9,8},{10,9},{11,1... | collective-permute-start | bytes 24968 | tf_op jit(solution)/shard_map/ppermute | solution.py:19
  404.7 7.3 collective-permute-start.4
  406.0 6.0 collective-permute-start.5
  420.5 8.5 %collective-permute-start.6 = (f32[4,260,2]{1,0,2:T(4,128)S(1)}, f32[4,260,2]{1,0,2:T(4,128)S(1)}, u32[]{:S(2)}, u32[]{:S(2)}) collective-permute-start(f32[4,260,2]{1,0,2:T(4,128)S(1)} %copy.192), channel_id=1, source_target_pairs={{0,1},{1,2},{2,3},{3,4},{4,5},{5,6},{6,7},{7,8},{8,9},{9,10},{10,1... | collective-permute-start | bytes 24968 | tf_op jit(solution)/shard_map/ppermute | solution.py:18
  421.4 7.9 %collective-permute-start.7 = (f32[4,260,2]{1,0,2:T(4,128)}, f32[4,260,2]{1,0,2:T(4,128)S(1)}, u32[]{:S(2)}, u32[]{:S(2)}) collective-permute-start(f32[4,260,2]{1,0,2:T(4,128)} %copy.193), channel_id=1, source_target_pairs={{1,0},{2,1},{3,2},{4,3},{5,4},{6,5},{7,6},{8,7},{9,8},{10,9},{11,1... | collective-permute-start | bytes 24968 | tf_op jit(solution)/shard_map/ppermute | solution.py:19
  455.2 138.3 %copy-start.6 = (f32[4,256,256]{2,0,1:T(4,128)}, f32[4,256,256]{2,0,1:T(4,128)S(1)}, u32[]{:S(2)}) copy-start(f32[4,256,256]{2,0,1:T(4,128)S(1)} %fusion.73) | copy-start | bytes 3145732
  511.9 81.6 %copy-start.24 = (f32[4,128,128]{2,0,1:T(4,128)S(1)}, f32[4,128,128]{2,0,1:T(4,128)}, u32[]{:S(2)}) copy-start(f32[4,128,128]{2,0,1:T(4,128)} %add_multiply_fusion.12) | copy-start | bytes 786436
  593.6 16.3 %copy-start.44 = (f32[1,128,128]{2,0,1:T(1,128)S(1)}, f32[1,128,128]{2,0,1:T(1,128)}, u32[]{:S(2)}) copy-start(f32[1,128,128]{2,0,1:T(1,128)} %get-tuple-element.152) | copy-start | bytes 196612
  595.0 14.9 %collective-permute-start.8 = (f32[10,128,128]{2,1,0:T(8,128)S(1)}, f32[10,128,128]{2,1,0:T(8,128)S(1)}, u32[]{:S(2)}, u32[]{:S(2)}) collective-permute-start(f32[10,128,128]{2,1,0:T(8,128)S(1)} %copy.204), channel_id=1, source_target_pairs={{0,16},{16,0},{32,48},{48,32},{64,80},{80,64},{96,112},{112,96},{1... | collective-permute-start | bytes 1966088 | tf_op jit(solution)/shard_map/ppermute | solution.py:31
  612.2 3.2 collective-permute-start.9
  618.3 9.9 %copy-start = (f32[10,256,128]{2,0,1:T(8,128)}, f32[10,256,128]{2,0,1:T(8,128)S(1)}, u32[]{:S(2)}) copy-start(f32[10,256,128]{2,0,1:T(8,128)S(1)} %get-tuple-element.68) | copy-start | bytes 3932164
  618.3 7.3 collective-permute-start.10
  619.9 5.8 collective-permute-start.11
  625.6 5.3 collective-permute-start.12
  641.7 10.7 %collective-permute-start.13 = (f32[4,260,2]{1,0,2:T(4,128)S(1)}, f32[4,260,2]{1,0,2:T(4,128)S(1)}, u32[]{:S(2)}, u32[]{:S(2)}) collective-permute-start(f32[4,260,2]{1,0,2:T(4,128)S(1)} %copy.210), channel_id=1, source_target_pairs={{0,1},{1,2},{2,3},{3,4},{4,5},{5,6},{6,7},{7,8},{8,9},{9,10},{10,1... | collective-permute-start | bytes 24968 | tf_op jit(solution)/shard_map/ppermute | solution.py:18
  643.0 10.5 %collective-permute-start.14 = (f32[4,260,2]{1,0,2:T(4,128)S(1)}, f32[4,260,2]{1,0,2:T(4,128)S(1)}, u32[]{:S(2)}, u32[]{:S(2)}) collective-permute-start(f32[4,260,2]{1,0,2:T(4,128)S(1)} %copy.211), channel_id=1, source_target_pairs={{1,0},{2,1},{3,2},{4,3},{5,4},{6,5},{7,6},{8,7},{9,8},{10,9},{11,1... | collective-permute-start | bytes 24968 | tf_op jit(solution)/shard_map/ppermute | solution.py:19
  655.8 3.2 collective-permute-start.15
  679.6 11.6 %copy-start.7 = (f32[4,256,256]{2,0,1:T(4,128)S(1)}, f32[4,256,256]{2,0,1:T(4,128)}, u32[]{:S(2)}) copy-start(f32[4,256,256]{2,0,1:T(4,128)} %copy-done.6) | copy-start | bytes 3145732
  680.6 7.3 collective-permute-start.16
  683.0 5.2 collective-permute-start.17
  688.1 5.2 collective-permute-start.18
  701.3 7.9 %collective-permute-start.19 = (f32[4,260,2]{1,0,2:T(4,128)S(1)}, f32[4,260,2]{1,0,2:T(4,128)}, u32[]{:S(2)}, u32[]{:S(2)}) collective-permute-start(f32[4,260,2]{1,0,2:T(4,128)S(1)} %copy.216), channel_id=1, source_target_pairs={{0,1},{1,2},{2,3},{3,4},{4,5},{5,6},{6,7},{7,8},{8,9},{9,10},{10,1... | collective-permute-start | bytes 24968 | tf_op jit(solution)/shard_map/ppermute | solution.py:18
  701.7 9.4 %collective-permute-start.20 = (f32[4,260,2]{1,0,2:T(4,128)S(1)}, f32[4,260,2]{1,0,2:T(4,128)}, u32[]{:S(2)}, u32[]{:S(2)}) collective-permute-start(f32[4,260,2]{1,0,2:T(4,128)S(1)} %copy.217), channel_id=1, source_target_pairs={{1,0},{2,1},{3,2},{4,3},{5,4},{6,5},{7,6},{8,7},{9,8},{10,9},{11,1... | collective-permute-start | bytes 24968 | tf_op jit(solution)/shard_map/ppermute | solution.py:19
  714.0 2.2 collective-permute-start.21
  (38 other events, 140.2 us)
where the time goes:
time: 758 us; the launch traced here: 747 us
  local copies, waits for them, and re-layouts  523 us (69%)
  other arithmetic  153 us (20%)
  starting transfers between devices  46.4 us (6%)
  waiting for transfers between devices  22.5 us (3%)
    slice x4, local copies, waits for them, and re-layouts, coarse(): field[:, 1::2, 1::2]  140 us
    slice x4, local copies, waits for them, and re-layouts, coarse(): field[:, 1::2, 0::2]  119 us
    slice x4, local copies, waits for them, and re-layouts, coarse(): field[:, 0::2, 0::2] + field[:, 1::2, 0::2] + field[:, 0::2, 1::2]  113 us
    slice x4, local copies, waits for them, and re-layouts, coarse(): field[:, 0::2, 1::2]  113 us
    ppermute x8, starting transfers between devices, with_halo(): after = lax.ppermute(first, axis, down)  29.7 us
    add x8, other arithmetic, sweep(): spectral = jnp.abs(normal_speed) + jnp.sqrt(1.4 * pressure * inverse)  29.5 us
    sub x8, other arithmetic, sweep(): face_flux = central - face_spectral * damping  28 us
    ppermute x6, waiting for transfers between devices, swapped(): return lax.ppermute(block, axis, route)  18.5 us
  transfers between devices with their start and end apart: 22, of which 9 were waited for; matrix products, arithmetic and copies ran while one was open for 36% of the time, Pallas kernels for 0%

commit v1 on v0

v1 whole, which is shorter than its diff:
```python
import jax
import jax.numpy as jnp
from jax import lax
from jax.experimental import pallas as pl
from jax.experimental.pallas import tpu as pltpu
from jax.sharding import PartitionSpec as P

MESH = pl.DeviceIdType.MESH
LANES = 128
SUB = 8
HALO = 8
STRIP = 24

WINF_R = (1.0, 0.5, 0.0, 1.0 / 0.56 + 0.125)
WINF_C = (1.0, 0.0, 0.5, 1.0 / 0.56 + 0.125)


def lane_index():
    return lax.broadcasted_iota(jnp.int32, (SUB, LANES), 1)


def lane_roll(v, shift):
    return pltpu.roll(v, shift % LANES, 1)


def sub_roll(v, shift):
    return pltpu.roll(v, shift % SUB, 0)


def shift_pair(vals, k):
    lane = lane_index()
    a, b = (lane_roll(v, -k) for v in vals)
    inside = lane < LANES - 1 if k == 1 else lane > 0
    return [jnp.where(inside, a, b), jnp.where(inside, b, a)]


def shift_packed(vals, k):
    lane = lane_index()
    (v,) = vals
    if k == 1:
        return [jnp.where(lane >= LANES - 2, lane_roll(v, -3), lane_roll(v, -2))]
    return [jnp.where(lane < 2, lane_roll(v, 3), lane_roll(v, 2))]


def make_strip_shift(step):
    def shift(vals, k):
        lane = lane_index()
        (v,) = vals
        a = lane_roll(v, -k * step)
        b = sub_roll(a, -2 * k)
        outside = lane >= LANES - step if k == 1 else lane < step
        return [jnp.where(outside, b, a)]

    return shift


shift_strip = make_strip_shift(1)
shift_strip_coarse = make_strip_shift(2)


def loop(lo, hi, unroll, body):
    count = hi - lo
    while count % unroll:
        unroll -= 1

    def run(step, carry):
        for i in range(unroll):
            carry = body(lo + step * unroll + i, carry)
        return carry

    return lambda carry: lax.fori_loop(0, count // unroll, run, carry)


def primitives(w_ref, p_ref, tiles, lo, hi, unroll=4):
    def body(r, carry):
        for t in range(tiles):
            density, mom_r, mom_l, energy = (w_ref[t, c, r] for c in range(4))
            inverse = 1.0 / density
            u = mom_r * inverse
            v = mom_l * inverse
            press = 0.4 * (energy - 0.5 * (mom_r * u + mom_l * v))
            p_ref[t, 0, r] = press
            p_ref[t, 1, r] = u
            p_ref[t, 2, r] = v
            p_ref[t, 3, r] = jnp.sqrt(1.4 * press * inverse)
        return carry

    loop(lo, hi, unroll, body)(0)


def face_coefs(sensor_a, sensor_b, spec_a, spec_b):
    second = jnp.maximum(sensor_a, sensor_b)
    fourth = jnp.maximum(0.0, 1.0 / 32.0 - second)
    total = spec_a + spec_b
    coef_b = total * fourth
    coef_a = total * second + 2.0 * coef_b
    return coef_a, coef_b


def quarter_sensor(low, mid, high):
    ends = low + high
    twice = 2.0 * mid
    return 0.25 * jnp.abs(ends - twice) / (ends + twice)


def along_rows(w_ref, p_ref, d_ref, tiles, lo, hi, unroll=8):
    def flux(t, r):
        w = [w_ref[t, c, r] for c in range(4)]
        press, q, sound = p_ref[t, 0, r], p_ref[t, 1, r], p_ref[t, 3, r]
        f = [w[1], w[1] * q + press, w[2] * q, (w[3] + press) * q]
        return f, jnp.abs(q) + sound

    def sensor(t, r):
        return quarter_sensor(p_ref[t, 0, r - 1], p_ref[t, 0, r], p_ref[t, 0, r + 1])

    def diff(t, r):
        return [w_ref[t, c, r + 1] - w_ref[t, c, r] for c in range(4)]

    def face(t, r, d_back, d_here, f_here, s_here, n_here):
        d_next = diff(t, r + 1)
        f_next, s_next = flux(t, r + 1)
        n_next = sensor(t, r + 1)
        ca, cb = face_coefs(n_here, n_next, s_here, s_next)
        h = [
            f_here[c] + f_next[c] - ca * d_here[c] + cb * (d_next[c] + d_back[c])
            for c in range(4)
        ]
        return h, d_next, f_next, s_next, n_next

    for t in range(tiles):
        d_back = diff(t, lo - 2)
        d_here = diff(t, lo - 1)
        f_here, s_here = flux(t, lo - 1)
        n_here = sensor(t, lo - 1)
        h, d_next, f_next, s_next, n_next = face(t, lo - 1, d_back, d_here, f_here, s_here, n_here)

        def body(r, carry):
            h_back, d_back, d_here, f_here, s_here, n_here = carry
            h, d_next, f_next, s_next, n_next = face(t, r, d_back, d_here, f_here, s_here, n_here)
            for c in range(4):
                d_ref[t, c, r] = h[c] - h_back[c]
            return h, d_here, d_next, f_next, s_next, n_next

        loop(lo, hi, unroll, body)((h, d_here, d_next, f_next, s_next, n_next))


def along_lanes(w_ref, p_ref, d_ref, tiles, lo, hi, shift, emit, unroll=2):
    every = range(tiles)

    def body(r, carry):
        w = [[w_ref[t, c, r] for t in every] for c in range(4)]
        press = [p_ref[t, 0, r] for t in every]
        q = [p_ref[t, 2, r] for t in every]
        spec = [jnp.abs(q[t]) + p_ref[t, 3, r] for t in every]
        w_up = [shift(w[c], 1) for c in range(4)]
        p_up, p_down = shift(press, 1), shift(press, -1)
        q_up = shift(q, 1)
        s_up = shift(spec, 1)
        sens = [quarter_sensor(p_down[t], press[t], p_up[t]) for t in every]
        n_up = shift(sens, 1)
        coefs = [face_coefs(sens[t], n_up[t], spec[t], s_up[t]) for t in every]
        out = []
        for c in range(4):
            d = [w_up[c][t] - w[c][t] for t in every]
            d_up, d_down = shift(d, 1), shift(d, -1)
            h = []
            for t in every:
                if c == 0:
                    f = w[2][t] + w_up[2][t]
                elif c == 1:
                    f = w[1][t] * q[t] + w_up[1][t] * q_up[t]
                elif c == 2:
                    f = (w[2][t] * q[t] + press[t]) + (w_up[2][t] * q_up[t] + p_up[t])
                else:
                    f = (w[3][t] + press[t]) * q[t] + (w_up[3][t] + p_up[t]) * q_up[t]
                h.append(f - coefs[t][0] * d[t] + coefs[t][1] * (d_up[t] + d_down[t]))
            h_down = shift(h, -1)
            out.append([(h[t] - h_down[t]) + d_ref[t, c, r] for t in every])
        emit(r, w, out)
        return carry

    loop(lo, hi, unroll, body)(0)


def with_source(w, total, wall, far, winf, half_h, h_square):
    if h_square != 1.0:
        wall, far = h_square * wall, h_square * far
    both = 2.0 * wall + far
    out = []
    for c in range(4):
        base = total[c] if half_h == 1.0 else half_h * total[c]
        weight = both if c in (1, 2) else far
        term = weight * w[c]
        if winf[c] != 0.0:
            term = term - far * winf[c]
        out.append(base + term)
    return out


def spectral_sum(p_ref, t, r):
    return jnp.abs(p_ref[t, 1, r]) + jnp.abs(p_ref[t, 2, r]) + 2.0 * p_ref[t, 3, r]


def leg(refs, tiles, shift, shift_coarse, restrict_lanes, winf, rows, refresh, coarse_tiles=1):
    w, pr, dx, sm, fr, kind, cs, cpr, cdx, csum, kk, seg, forc, corr, share = refs
    (p1, s1, p2, s2, c_state, c_seg, c_out) = rows

    def smooth(r, w_vals, total):
        for t in range(tiles):
            wall = jnp.where(kind[t, r] == 1.0, 1.0, 0.0)
            far = jnp.where(kind[t, r] == 2.0, 1.0, 0.0)
            mine = [w_vals[c][t] for c in range(4)]
            res = with_source(mine, [total[c][t] for c in range(4)], wall, far, winf, 0.5, 1.0)
            scale = 0.4 / spectral_sum(pr, t, r)
            for c in range(4):
                sm[t, c, r] = mine[c] - scale * res[c]

    def fine(r, w_vals, total):
        for t in range(tiles):
            wall = jnp.where(kind[t, r] == 1.0, 1.0, 0.0)
            far = jnp.where(kind[t, r] == 2.0, 1.0, 0.0)
            mine = [w_vals[c][t] for c in range(4)]
            res = with_source(mine, [total[c][t] for c in range(4)], wall, far, winf, 0.5, 1.0)
            for c in range(4):
                fr[t, c, r] = res[c]

    primitives(w, pr, tiles, *p1)
    along_rows(w, pr, dx, tiles, *s1)
    yield "rows"
    along_lanes(w, pr, dx, tiles, *s1, shift, smooth)
    refresh(sm, tiles)
    yield "smoothed"
    primitives(sm, pr, tiles, *p2)
    along_rows(sm, pr, dx, tiles, *s2)
    along_lanes(sm, pr, dx, tiles, *s2, shift, fine)
    yield "fine"

    def state(k, carry):
        for c in range(4):
            cs[0, c, k] = 0.25 * restrict_lanes([sm[t, c, 2 * k + off] + sm[t, c, 2 * k + off + 1] for t in range(tiles)])
        return carry

    off = -2 if tiles == 2 else 0
    loop(*c_state, 2, state)(0)
    refresh(cs, 1)

    def sums(k, carry):
        for c in range(4):
            csum[0, c, k] = restrict_lanes([fr[t, c, 2 * k + off] + fr[t, c, 2 * k + off + 1] for t in range(tiles)])
        for i, code in enumerate((1.0, 2.0)):
            share[0, i, k] = 0.25 * restrict_lanes(
                [
                    jnp.where(kind[t, 2 * k + off] == code, 1.0, 0.0)
                    + jnp.where(kind[t, 2 * k + off + 1] == code, 1.0, 0.0)
                    for t in range(tiles)
                ]
            )
        return carry

    loop(*c_seg, 2, sums)(0)
    wide = (0, 20) if tiles == 2 else c_seg
    primitives(cs, cpr, 1, *wide)

    def segment(k, carry):
        scale = 0.2 / spectral_sum(cpr, 0, k)
        kk[0, k] = scale
        for c in range(4):
            seg[0, c, k] = cs[0, c, k] - scale * csum[0, c, k]
        return carry

    loop(*c_seg, 4, segment)(0)
    refresh(seg, 1)

    def force(k, w_vals, total):
        res = with_source([v[0] for v in w_vals], [v[0] for v in total], share[0, 0, k], share[0, 1, k], winf, 1.0, 4.0)
        for c in range(4):
            forc[0, c, k] = csum[0, c, k] - res[c]

    along_rows(cs, cpr, cdx, 1, *c_out)
    along_lanes(cs, cpr, cdx, 1, *c_out, shift_coarse, force)
    primitives(seg, cpr, 1, *wide)

    def final(k, w_vals, total):
        res = with_source([v[0] for v in w_vals], [v[0] for v in total], share[0, 0, k], share[0, 1, k], winf, 1.0, 4.0)
        for c in range(4):
            corr[0, c, k] = -kk[0, k] * (res[c] + forc[0, c, k])

    along_rows(seg, cpr, cdx, 1, *c_out)
    along_lanes(seg, cpr, cdx, 1, *c_out, shift_coarse, final)
    yield "done"


MAIN_ROWS = ((0, 36), (2, 34), (0, 36), (2, 34), (2, 18), (2, 18), (2, 18))
STRIP_ROWS = ((0, 24), (2, 22), (2, 22), (4, 20), (1, 11), (2, 10), (4, 8))


def restrict_pair(vals):
    lane = lane_index()
    a, b = vals
    return jnp.where(lane % 2 == 0, a + lane_roll(a, -1), b + lane_roll(b, 1))


def restrict_strip(vals):
    lane = lane_index()
    (a,) = vals
    return a + jnp.where(lane % 2 == 0, lane_roll(a, -1), lane_roll(a, 1))


def refresh_main(ref, tiles):
    depth = ref.shape[2]
    for t in range(tiles):
        for c in range(4):
            for i in range(2):
                ref[t, c, i] = sub_roll(ref[t, c, depth - 4 + i], 1)
                ref[t, c, depth - 2 + i] = sub_roll(ref[t, c, 2 + i], -1)


def no_refresh(ref, tiles):
    pass


def run_to(steps, name):
    for reached in steps:
        if reached == name:
            return


T_L, B_L, T_0, B_0, T_1, B_1, T_R, B_R = range(8)
L_0, R_0, L_1, R_1 = range(4)


def kernel(nx, ny, flow_hbm, kind_hbm, new_hbm, res_hbm, inb, kb, rowbuf, rowkind, colbuf, pack, got, out_new, out_res,
           row_out, col_out, *rest):
    main_refs, strip_refs, (load_sem, send_sem, recv_sem, store_sem) = rest[:15], rest[15:30], rest[30:]
    gx, gy = lax.axis_index("gx"), lax.axis_index("gy")
    up, down = lax.rem(gx + nx - 1, nx), lax.rem(gx + 1, nx)
    left, right = lax.rem(gy + ny - 1, ny), lax.rem(gy + 1, ny)
    neighbours = [(up, gy), (down, gy), (gx, left), (gx, right), (up, left), (up, right), (down, left), (down, right)]

    loads = []
    for t in range(2):
        cols = pl.ds(t * LANES, LANES)
        loads.append(pltpu.make_async_copy(flow_hbm.at[:, :, cols], inb.at[t], load_sem.at[2 * t]))
        loads.append(pltpu.make_async_copy(kind_hbm.at[:, cols], kb.at[t], load_sem.at[2 * t + 1]))
    for copy in loads:
        copy.start()

    barrier = pltpu.get_barrier_semaphore()
    for where in neighbours:
        pl.semaphore_signal(barrier, inc=1, device_id=where, device_id_type=MESH)
    for copy in loads:
        copy.wait()

    lane = lane_index()

    for side in range(2):
        for i, row in enumerate((0, 8, 240, 248)):
            rows = pl.ds(row, 8)
            total = None
            for c in range(5):
                v = kb[side, rows, :].astype(jnp.float32) if c == 4 else inb[side, c, rows, :]
                if side:
                    v = lane_roll(v, -8 * c)
                    total = v if c == 0 else jnp.where(lane < LANES - 8 * c, v, total)
                else:
                    v = lane_roll(v, 8 * c)
                    total = v if c == 0 else jnp.where(lane >= 8 * c, v, total)
            pack[side, pl.ds(8 * i, 8), :] = total

    for c, source in enumerate((0, 2, 1, 3, 4)):
        for side in range(2):
            for half in range(2):
                rows = pl.ds(half * LANES, LANES)
                v = kb[side, rows, :].astype(jnp.float32) if c == 4 else inb[side, source, rows, :]
                turned = v.T
                seg = half * 2 + side
                if side:
                    colbuf[c, pl.ds(seg * STRIP, 16), :] = turned[112:128]
                else:
                    colbuf[c, pl.ds(seg * STRIP + 8, 16), :] = turned[0:16]

    for t, (top, bottom) in enumerate(((T_0, B_0), (T_1, B_1))):
        for c in range(4):
            rowbuf[c, pl.ds(top * STRIP + 8, 16), :] = inb[t, c, pl.ds(0, 16), :]
            rowbuf[c, pl.ds(bottom * STRIP, 16), :] = inb[t, c, pl.ds(240, 16), :]
        rowbuf[4, pl.ds(top * STRIP + 8, 16), :] = kb[t, pl.ds(0, 16), :].astype(jnp.float32)
        rowbuf[4, pl.ds(bottom * STRIP, 16), :] = kb[t, pl.ds(240, 16), :].astype(jnp.float32)

    w_main, kind_main = main_refs[0], main_refs[5]

    def relayout(r, carry):
        for t in range(2):
            for c in range(4):
                w_main[t, c, r + 2] = inb[t, c, pl.ds(r, SUB, stride=32), :]
            kind_main[t, r + 2] = kb[t, pl.ds(r, SUB, stride=32), :].astype(jnp.float32)
        return carry

    loop(0, 32, 4, relayout)(0)
    refresh_main(w_main, 2)

    main = leg(main_refs, 2, shift_pair, shift_packed, restrict_pair, WINF_R, MAIN_ROWS, refresh_main)
    run_to(main, "rows")

    pl.semaphore_wait(barrier, 8)
    number = 0
    copies = []

    def send(src, dst, where):
        nonlocal number
        copy = pltpu.make_async_remote_copy(
            src_ref=src, dst_ref=dst, send_sem=send_sem.at[number], recv_sem=recv_sem.at[number],
            device_id=where, device_id_type=MESH)
        copy.start()
        copies.append(copy)
        number += 1

    low, high = pl.ds(0, 8), pl.ds(248, 8)
    send(pack.at[1, pl.ds(24, 8)], got.at[0, pl.ds(0, 8)], (down, right))
    send(pack.at[0, pl.ds(24, 8)], got.at[1, pl.ds(0, 8)], (down, left))
    send(pack.at[1, pl.ds(0, 8)], got.at[0, pl.ds(40, 8)], (up, right))
    send(pack.at[0, pl.ds(0, 8)], got.at[1, pl.ds(40, 8)], (up, left))
    for t, (top, bottom) in enumerate(((T_0, B_0), (T_1, B_1))):
        send(inb.at[t, :, high, :], rowbuf.at[pl.ds(0, 4), pl.ds(top * STRIP, 8), :], (down, gy))
        send(inb.at[t, :, low, :], rowbuf.at[pl.ds(0, 4), pl.ds(bottom * STRIP + 16, 8), :], (up, gy))
    send(kb.at[:, high, :], rowkind.at[0], (down, gy))
    send(kb.at[:, low, :], rowkind.at[1], (up, gy))
    send(pack.at[1], got.at[0, pl.ds(8, 32)], (gx, right))
    send(pack.at[0], got.at[1, pl.ds(8, 32)], (gx, left))
    first_column = number
    for to_left, to_right in ((L_0, R_0), (L_1, R_1)):
        send(colbuf.at[:, pl.ds(to_right * STRIP + 8, 8), :], colbuf.at[:, pl.ds(to_left * STRIP, 8), :], (gx, right))
        send(colbuf.at[:, pl.ds(to_left * STRIP + 8, 8), :], colbuf.at[:, pl.ds(to_right * STRIP + 16, 8), :], (gx, left))

    run_to(main, "done")
    sm_main, fr_main, corr_main = main_refs[3], main_refs[4], main_refs[13]

    def finish(k, carry):
        for c in range(4):
            v = corr_main[0, c, k + 2]
            even = lane_index() % 2 == 0
            add = [jnp.where(even, v, lane_roll(v, 1)), jnp.where(even, lane_roll(v, -1), v)]
            for t in range(2):
                for i in range(2):
                    r = 2 * k + i
                    out_new[t, c, pl.ds(r, SUB, stride=32), :] = sm_main[t, c, r + 2] + add[t]
                    out_res[t, c, pl.ds(r, SUB, stride=32), :] = fr_main[t, c, r + 2]
        return carry

    loop(0, 16, 2, finish)(0)

    w_strip, sm_strip, fr_strip, kind_strip, corr_strip = (strip_refs[i] for i in (0, 3, 4, 5, 13))

    def gather(buf):
        def body(r, carry):
            for c in range(4):
                w_strip[0, c, r] = buf[c, pl.ds(r, SUB, stride=STRIP), :]
            kind_strip[0, r] = buf[4, pl.ds(r, SUB, stride=STRIP), :]
            return carry

        loop(0, STRIP, 4, body)(0)

    for copy in copies[first_column:]:
        copy.wait_recv()
    gather(colbuf)
    run_to(leg(strip_refs, 1, shift_strip, shift_strip_coarse, restrict_strip, WINF_C, STRIP_ROWS, no_refresh), "done")

    def column_out(i, carry):
        for c, target in enumerate((0, 2, 1, 3)):
            col_out[pl.ds(target * 8 + i, SUB, stride=64), :] = sm_strip[0, c, i + 8] + corr_strip[0, c, (i + 8) // 2]
            col_out[pl.ds((target + 4) * 8 + i, SUB, stride=64), :] = fr_strip[0, c, i + 8]
        return carry

    loop(0, 8, 2, column_out)(0)
    for half in range(2):
        turned = col_out[pl.ds(half * LANES, LANES), :].T

        for a in range(8):
            ref, c = (out_new, a) if a < 4 else (out_res, a - 4)
            rows = pl.ds(half * LANES, LANES)
            wide = lax.broadcasted_iota(jnp.int32, (LANES, LANES), 1)
            ref[0, c, rows, :] = jnp.where(wide < 8, pltpu.roll(turned, (-8 * a) % LANES, 1), ref[0, c, rows, :])
            ref[1, c, rows, :] = jnp.where(wide >= 120, pltpu.roll(turned, (56 - 8 * a) % LANES, 1), ref[1, c, rows, :])

    stores = []

    def store(src, dst):
        copy = pltpu.make_async_copy(src, dst, store_sem.at[len(stores)])
        copy.start()
        stores.append(copy)

    inner = pl.ds(8, 240)
    for t in range(2):
        cols = pl.ds(t * LANES, LANES)
        store(out_new.at[t, :, inner, :], new_hbm.at[:, inner, cols])
        store(out_res.at[t, :, inner, :], res_hbm.at[:, inner, cols])

    for copy in copies[:first_column]:
        copy.wait_recv()
    for side, (top, bottom) in enumerate(((T_L, B_L), (T_R, B_R))):
        for j, seg in enumerate((top, bottom)):
            for i in range(3):
                v = got[side, pl.ds(24 * j + 8 * i, 8), :]
                for c in range(5):
                    rowbuf[c, pl.ds(seg * STRIP + 8 * i, 8), :] = lane_roll(v, -8 * c if side else 8 * c)
    for t, (top, bottom) in enumerate(((T_0, B_0), (T_1, B_1))):
        rowbuf[4, pl.ds(top * STRIP, 8), :] = rowkind[0, t].astype(jnp.float32)
        rowbuf[4, pl.ds(bottom * STRIP + 16, 8), :] = rowkind[1, t].astype(jnp.float32)
    gather(rowbuf)
    run_to(leg(strip_refs, 1, shift_strip, shift_strip_coarse, restrict_strip, WINF_R, STRIP_ROWS, no_refresh), "done")

    def row_result(i, carry):
        for c in range(4):
            row_out[0, c, pl.ds(i, SUB, stride=8), :] = sm_strip[0, c, i + 8] + corr_strip[0, c, (i + 8) // 2]
            row_out[1, c, pl.ds(i, SUB, stride=8), :] = fr_strip[0, c, i + 8]
        return carry

    loop(0, 8, 2, row_result)(0)
    for a, out in enumerate((new_hbm, res_hbm)):
        for t, (top, bottom) in enumerate(((T_0, B_0), (T_1, B_1))):
            cols = pl.ds(t * LANES, LANES)
            store(row_out.at[a, :, pl.ds(top * 8, 8), :], out.at[:, low, cols])
            store(row_out.at[a, :, pl.ds(bottom * 8, 8), :], out.at[:, high, cols])
    for copy in copies:
        copy.wait_send()
    for copy in stores:
        copy.wait()


def vmem(*shape):
    return pltpu.VMEM(shape, jnp.float32)


def domain(tiles, rows, coarse_rows):
    tile = (SUB, LANES)
    return [
        vmem(tiles, 4, rows, *tile),
        vmem(tiles, 4, rows, *tile),
        vmem(tiles, 4, rows, *tile),
        vmem(tiles, 4, rows, *tile),
        vmem(tiles, 4, rows, *tile),
        vmem(tiles, rows, *tile),
        vmem(1, 4, coarse_rows, *tile),
        vmem(1, 4, coarse_rows, *tile),
        vmem(1, 4, coarse_rows, *tile),
        vmem(1, 4, coarse_rows, *tile),
        vmem(1, coarse_rows, *tile),
        vmem(1, 4, coarse_rows, *tile),
        vmem(1, 4, coarse_rows, *tile),
        vmem(1, 4, coarse_rows, *tile),
        vmem(1, 2, coarse_rows, *tile),
    ]


def solution(mesh):
    nx, ny = mesh.shape["gx"], mesh.shape["gy"]

    def local(flow_state, cell_kind):
        import functools

        out = jax.ShapeDtypeStruct(flow_state.shape, jnp.float32)
        hbm = pl.BlockSpec(memory_space=pl.ANY)
        return pl.pallas_call(
            functools.partial(kernel, nx, ny),
            out_shape=(out, out),
            in_specs=[hbm, hbm],
            out_specs=(hbm, hbm),
            scratch_shapes=[
                vmem(2, 4, 256, LANES),
                pltpu.VMEM((2, 256, LANES), jnp.int32),
                vmem(5, 8 * STRIP, LANES),
                pltpu.VMEM((2, 2, 8, LANES), jnp.int32),
                vmem(5, 8 * STRIP, LANES),
                vmem(2, 32, LANES),
                vmem(2, 48, LANES),
                vmem(2, 4, 256, LANES),
                vmem(2, 4, 256, LANES),
                vmem(2, 4, 64, LANES),
                vmem(512, LANES),
                *domain(2, 36, 20),
                *domain(1, 24, 12),
                pltpu.SemaphoreType.DMA((4,)),
                pltpu.SemaphoreType.DMA((16,)),
                pltpu.SemaphoreType.DMA((16,)),
                pltpu.SemaphoreType.DMA((12,)),
            ],
            compiler_params=pltpu.CompilerParams(collective_id=0, has_side_effects=True),
        )(flow_state, cell_kind)

    return jax.shard_map(
        local,
        mesh=mesh,
        in_specs=(P(None, "gx", "gy"), P("gx", "gy")),
        out_specs=(P(None, "gx", "gy"), P(None, "gx", "gy")),
        check_vma=False,
    )
```

time: 758 us -> 46.7 us (0.06); the launches traced: 747 us -> 46.6 us
  local copies, waits for them, and re-layouts: 523 us -> 3.35 us
  other arithmetic: 153 us -> 0 us
  starting transfers between devices: 46.4 us -> 0 us
  Pallas kernels: 0 us -> 42.6 us
  waiting for transfers between devices: 22.5 us -> 0 us
    slice x39 -> x0, local copies, waits for them, and re-layouts: 502 us -> none  [the longest x4 140 us: coarse(): field[:, 1::2, 1::2]]
    add x19 -> x0, other arithmetic: 47.4 us -> none  [the longest x8 29.5 us: sweep(): spectral = jnp.abs(normal_speed) + jnp.sqrt(1.4 * pressure * inverse)]
    ppermute x22 -> x0, starting transfers between devices: 46.4 us -> none  [the longest x8 29.7 us: with_halo(): after = lax.ppermute(first, axis, down)]
    pallas_call x0 -> x1, Pallas kernels: none -> 42.6 us  [local(): pl.pallas_call(functools.partial(kernel, nx, ny), out_shape=(out, out), i...]
    sub x10 -> x0, other arithmetic: 32.1 us -> none  [the longest x8 28 us: sweep(): face_flux = central - face_spectral * damping]
    concatenate x19 -> x0, other arithmetic: 23.7 us -> none  [the longest x4 9.55 us: sweep(): jnp.concatenate([momentum_x, momentum_x * speed_x + pressure, momentum_y...]
    ppermute x22 -> x0, waiting for transfers between devices: 22.5 us -> none  [the longest x6 18.5 us: swapped(): return lax.ppermute(block, axis, route)]
    mul x13 -> x0, other arithmetic: 14.4 us -> none  [the longest x8 9.06 us: sweep(): 0.5 * (section(spectral, 1, length + 2, axis_dim) + section(spectral, 2,...]
  transfers between devices with their start and end apart: 22 -> 0, of which waited for: 9 -> 0; matrix products, arithmetic and copies ran while one was open for 36% -> 0% of each run, Pallas kernels for 0% -> 0%
where the time goes in v1:
time: 46.7 us; the launch traced here: 46.6 us
  Pallas kernels  42.6 us (91%)
  local copies, waits for them, and re-layouts  3.35 us (7%)
  between operations  0.65 us (1%)
    pallas_call x1, Pallas kernels, local(): pl.pallas_call(functools.partial(kernel, nx, ny), out_shape=(out, out), i...  42.6 us
    unnamed x4, local copies, waits for them, and re-layouts  3.35 us

profile of v1, /device:TPU:0, one launch (start us, length us, event | category | flops | bytes accessed | tf_op | source)
XLA Modules:
  0.0 46.6 jit_solution(2860813067969427267)
XLA Ops:
  0.6 42.6 %shard_map.41 = (f32[4,256,256]{2,1,0:T(8,128)}, f32[4,256,256]{2,1,0:T(8,128)}) custom-call(f32[4,256,256]{2,1,0:T(8,128)} %flow_hbm.1, s32[256,256]{1,0:T(8,128)} %kind_hbm.1), custom_call_target="tpu_custom_call" | custom-call | tf_op jit(solution)/shard_map/pallas_call | solution.py:562
  43.2 0.0 copy-start
  43.2 2.4 %copy.6 = f32[4,256,256]{2,1,0:T(8,128)} copy(f32[4,256,256]{2,1,0:T(8,128)} %get-tuple-element.4) | data formatting | bytes 2097152
  45.6 0.0 copy-done
  45.6 1.0 %copy.7 = f32[4,256,256]{2,1,0:T(8,128)} copy(f32[4,256,256]{2,1,0:T(8,128)S(1)} %copy-done) | data formatting | bytes 2097152
Async XLA Ops:
  43.2 2.4 %copy-start = (f32[4,256,256]{2,1,0:T(8,128)S(1)}, f32[4,256,256]{2,1,0:T(8,128)}, u32[]{:S(2)}) copy-start(f32[4,256,256]{2,1,0:T(8,128)} %get-tuple-element.5) | copy-start | bytes 3145732

commit v2 on v1

v2 whole, which is shorter than its diff:
```python
import functools

import jax
import jax.numpy as jnp
from jax import lax
from jax.experimental import pallas as pl
from jax.experimental.pallas import tpu as pltpu
from jax.sharding import PartitionSpec as P

MESH = pl.DeviceIdType.MESH
LANES = 128
SUB = 8
ROWS = 32
STRIP = 24

ENERGY = 1.0 / 0.56 + 0.125

LEFT, RIGHT, TOP_L, TOP, TOP_R, BOT_L, BOT, BOT_R = range(8)

FINE_UNROLL = 2
ROW_UNROLL = 8
COARSE_UNROLL = 4


def lane_index():
    return lax.broadcasted_iota(jnp.int32, (SUB, LANES), 1)


def sub_index():
    return lax.broadcasted_iota(jnp.int32, (SUB, LANES), 0)


def sub_roll(v, shift):
    return pltpu.roll(v, shift % SUB, 0)


def take(v, index):
    return jnp.take_along_axis(v, index, axis=1)


def ahead_main(v, k):
    return pltpu.roll(v, -k % LANES, 1)


def ahead_strip(v, k):
    here = pltpu.roll(v, -k % LANES, 1)
    lane = lane_index()
    if k > 0:
        return jnp.where(lane >= LANES - k, sub_roll(here, -1), here)
    return jnp.where(lane < -k, sub_roll(here, 1), here)


def loop(lo, hi, unroll, body, carry=0):
    count = hi - lo
    while count % unroll:
        unroll -= 1

    def run(step, carry):
        for i in range(unroll):
            carry = body(lo + step * unroll + i, carry)
        return carry

    return lax.fori_loop(0, count // unroll, run, carry)


def primitives(w_ref, p_ref, tiles, lo, hi, unroll=4):
    def body(r, carry):
        for t in range(tiles):
            density, mom_r, mom_l, energy = (w_ref[t, c, r] for c in range(4))
            inverse = 1.0 / density
            u = mom_r * inverse
            v = mom_l * inverse
            press = 0.4 * (energy - 0.5 * (mom_r * u + mom_l * v))
            p_ref[t, 0, r] = press
            p_ref[t, 1, r] = u
            p_ref[t, 2, r] = v
            p_ref[t, 3, r] = jnp.sqrt(1.4 * press * inverse)
        return carry

    loop(lo, hi, unroll, body)


def face_coefs(sensor_a, sensor_b, spec_a, spec_b):
    second = jnp.maximum(sensor_a, sensor_b)
    fourth = jnp.maximum(0.0, 1.0 / 32.0 - second)
    total = spec_a + spec_b
    coef_b = total * fourth
    coef_a = total * second + 2.0 * coef_b
    return coef_a, coef_b


def quarter_sensor(low, mid, high):
    ends = low + high
    twice = 2.0 * mid
    return 0.25 * jnp.abs(ends - twice) / (ends + twice)


def along_rows(w_ref, p_ref, d_ref, tiles, lo, hi, unroll):
    def flux(t, r):
        w = [w_ref[t, c, r] for c in range(4)]
        press, q, sound = p_ref[t, 0, r], p_ref[t, 1, r], p_ref[t, 3, r]
        f = [w[1], w[1] * q + press, w[2] * q, (w[3] + press) * q]
        return f, jnp.abs(q) + sound

    def sensor(t, r):
        return quarter_sensor(p_ref[t, 0, r - 1], p_ref[t, 0, r], p_ref[t, 0, r + 1])

    def diff(t, r):
        return [w_ref[t, c, r + 1] - w_ref[t, c, r] for c in range(4)]

    def face(t, r, d_back, d_here, f_here, s_here, n_here):
        d_next = diff(t, r + 1)
        f_next, s_next = flux(t, r + 1)
        n_next = sensor(t, r + 1)
        ca, cb = face_coefs(n_here, n_next, s_here, s_next)
        h = [
            f_here[c] + f_next[c] - ca * d_here[c] + cb * (d_next[c] + d_back[c])
            for c in range(4)
        ]
        return h, d_next, f_next, s_next, n_next

    for t in range(tiles):
        d_back = diff(t, lo - 2)
        d_here = diff(t, lo - 1)
        f_here, s_here = flux(t, lo - 1)
        n_here = sensor(t, lo - 1)
        h, d_next, f_next, s_next, n_next = face(t, lo - 1, d_back, d_here, f_here, s_here, n_here)

        def body(r, carry, t=t):
            h_back, d_back, d_here, f_here, s_here, n_here = carry
            h, d_next, f_next, s_next, n_next = face(t, r, d_back, d_here, f_here, s_here, n_here)
            for c in range(4):
                d_ref[t, c, r] = h[c] - h_back[c]
            return h, d_here, d_next, f_next, s_next, n_next

        loop(lo, hi, unroll, body, (h, d_here, d_next, f_next, s_next, n_next))


def lane_flux(w, press, q):
    return [w[2], w[1] * q, w[2] * q + press, (w[3] + press) * q]


def along_lanes_fine(w_ref, p_ref, d_ref, lo, hi, ahead, emit, unroll):
    def body(r, carry):
        we, wo = ([w_ref[t, c, r] for c in range(4)] for t in range(2))
        (pe, po), (qe, qo) = ([p_ref[t, i, r] for t in range(2)] for i in (0, 2))
        se, so = jnp.abs(qe) + p_ref[0, 3, r], jnp.abs(qo) + p_ref[1, 3, r]
        pe1, po1, pom = ahead(pe, 1), ahead(po, 1), ahead(po, -1)
        qe1, se1 = ahead(qe, 1), ahead(se, 1)
        we1 = [ahead(v, 1) for v in we]
        wo1 = [ahead(v, 1) for v in wo]
        wom = [ahead(v, -1) for v in wo]
        ne = quarter_sensor(pom, pe, po)
        no = quarter_sensor(pe, po, pe1)
        ne1 = quarter_sensor(po, pe1, po1)
        ae, be = face_coefs(ne, no, se, so)
        ao, bo = face_coefs(no, ne1, so, se1)
        fe, fo, fe1 = lane_flux(we, pe, qe), lane_flux(wo, po, qo), lane_flux(we1, pe1, qe1)
        out = []
        for c in range(4):
            de = wo[c] - we[c]
            do = we1[c] - wo[c]
            he = fe[c] + fo[c] - ae * de + be * (do + (we[c] - wom[c]))
            ho = fo[c] + fe1[c] - ao * do + bo * ((wo1[c] - we1[c]) + de)
            out.append([he - ahead(ho, -1) + d_ref[0, c, r], ho - he + d_ref[1, c, r]])
        for t, w in enumerate((we, wo)):
            emit(t, r, w, [out[c][t] for c in range(4)])
        return carry

    loop(lo, hi, unroll, body)


def along_lanes_coarse(w_ref, p_ref, d_ref, lo, hi, ahead, emit, unroll):
    def body(r, carry):
        w = [w_ref[0, c, r] for c in range(4)]
        press, q = p_ref[0, 0, r], p_ref[0, 2, r]
        spec = jnp.abs(q) + p_ref[0, 3, r]
        pm, p1, p2 = ahead(press, -1), ahead(press, 1), ahead(press, 2)
        q1, s1 = ahead(q, 1), ahead(spec, 1)
        wm, w1, w2 = ([ahead(v, k) for v in w] for k in (-1, 1, 2))
        ca, cb = face_coefs(quarter_sensor(pm, press, p1), quarter_sensor(press, p1, p2), spec, s1)
        f, f1 = lane_flux(w, press, q), lane_flux(w1, p1, q1)
        out = []
        for c in range(4):
            h = f[c] + f1[c] - ca * (w1[c] - w[c]) + cb * ((w2[c] - w1[c]) + (w[c] - wm[c]))
            out.append(h - ahead(h, -1) + d_ref[0, c, r])
        emit(0, r, w, out)
        return carry

    loop(lo, hi, unroll, body)


def with_source(w, total, both, far, winf, half_h):
    out = []
    for c in range(4):
        base = total[c] if half_h == 1.0 else half_h * total[c]
        term = (both if c in (1, 2) else far) * w[c]
        if not (isinstance(winf[c], float) and winf[c] == 0.0):
            term = term - far * winf[c]
        out.append(base + term)
    return out


def weights(kind):
    far = jnp.where(kind == 2.0, 1.0, 0.0)
    return jnp.where(kind == 1.0, 2.0, far), far


def spectral_sum(p_ref, t, r):
    return jnp.abs(p_ref[t, 1, r]) + jnp.abs(p_ref[t, 2, r]) + 2.0 * p_ref[t, 3, r]


def leg(refs, ahead, winf, rows, refresh, offset):
    w, pr, dx, sm, fr, cs, cpr, cdx, csum, kk, seg, forc, corr, share = refs
    (p1, s1, p2, s2, c_state, c_seg, c_prim, c_out) = rows

    def smooth(t, r, mine, total):
        both, far = weights(w[t, 4, r])
        res = with_source(mine, total, both, far, winf(), 0.5)
        scale = 0.4 / spectral_sum(pr, t, r)
        for c in range(4):
            sm[t, c, r] = mine[c] - scale * res[c]

    def fine(t, r, mine, total):
        both, far = weights(w[t, 4, r])
        res = with_source(mine, total, both, far, winf(), 0.5)
        for c in range(4):
            fr[t, c, r] = res[c]

    primitives(w, pr, 2, *p1)
    along_rows(w, pr, dx, 2, *s1, ROW_UNROLL)
    yield "rows"
    along_lanes_fine(w, pr, dx, *s1, ahead, smooth, FINE_UNROLL)
    refresh(sm)
    yield "smoothed"
    primitives(sm, pr, 2, *p2)
    along_rows(sm, pr, dx, 2, *s2, ROW_UNROLL)
    along_lanes_fine(sm, pr, dx, *s2, ahead, fine, FINE_UNROLL)
    yield "fine"

    def four(get, k):
        i = 2 * k + offset
        return (get(0, i) + get(0, i + 1)) + (get(1, i) + get(1, i + 1))

    def state(k, carry):
        for c in range(4):
            cs[0, c, k] = 0.25 * four(lambda t, i: sm[t, c, i], k)
        return carry

    loop(*c_state, 4, state)
    refresh(cs)

    def sums(k, carry):
        for c in range(4):
            csum[0, c, k] = four(lambda t, i: fr[t, c, i], k)
        for j in range(2):
            share[0, j, k] = four(lambda t, i: weights(w[t, 4, i])[j], k)
        return carry

    loop(*c_seg, 4, sums)
    primitives(cs, cpr, 1, *c_prim)

    def segment(k, carry):
        scale = 0.2 / spectral_sum(cpr, 0, k)
        kk[0, k] = scale
        for c in range(4):
            seg[0, c, k] = cs[0, c, k] - scale * csum[0, c, k]
        return carry

    loop(*c_seg, 4, segment)
    refresh(seg)

    def coarse_residual(k, mine, total):
        return with_source(mine, total, share[0, 0, k], share[0, 1, k], winf(), 1.0)

    def force(t, k, mine, total):
        res = coarse_residual(k, mine, total)
        for c in range(4):
            forc[0, c, k] = csum[0, c, k] - res[c]

    along_rows(cs, cpr, cdx, 1, *c_out, ROW_UNROLL)
    along_lanes_coarse(cs, cpr, cdx, *c_out, ahead, force, COARSE_UNROLL)
    primitives(seg, cpr, 1, *c_prim)

    def final(t, k, mine, total):
        res = coarse_residual(k, mine, total)
        for c in range(4):
            corr[0, c, k] = -kk[0, k] * (res[c] + forc[0, c, k])

    along_rows(seg, cpr, cdx, 1, *c_out, ROW_UNROLL)
    along_lanes_coarse(seg, cpr, cdx, *c_out, ahead, final, COARSE_UNROLL)
    yield "done"


MAIN_ROWS = ((0, 36), (2, 34), (0, 36), (2, 34), (2, 18), (2, 18), (0, 20), (2, 18))
STRIP_ROWS = ((0, 24), (2, 22), (2, 22), (4, 20), (2, 10), (2, 10), (2, 10), (4, 8))


def winf_main():
    return (1.0, 0.5, 0.0, ENERGY)


def winf_strip():
    column = sub_index() <= RIGHT
    return (1.0, jnp.where(column, 0.0, 0.5), jnp.where(column, 0.5, 0.0), ENERGY)


def refresh_main(ref):
    depth = ref.shape[2]
    for t in range(ref.shape[0]):
        for c in range(4):
            for i in range(2):
                ref[t, c, i] = sub_roll(ref[t, c, depth - 4 + i], 1)
                ref[t, c, depth - 2 + i] = sub_roll(ref[t, c, 2 + i], -1)


def no_refresh(ref):
    pass


def run_to(steps, name):
    for reached in steps:
        if reached == name:
            return


def kernel(nx, ny, flow_hbm, kind_hbm, out_new, out_res, raw, raw_kind, nat, nat_kind, columns, pack, got, col_in,
           col_turned, *rest):
    main_refs, strip_refs, sems = rest[:14], rest[14:28], rest[28:]
    load_sem, copy_sem, send_sem, recv_sem = sems
    gx, gy = lax.axis_index("gx"), lax.axis_index("gy")
    up, down = lax.rem(gx + nx - 1, nx), lax.rem(gx + 1, nx)
    left, right = lax.rem(gy + ny - 1, ny), lax.rem(gy + 1, ny)
    neighbours = [(up, gy), (down, gy), (gx, left), (gx, right), (up, left), (up, right), (down, left), (down, right)]
    barrier = pltpu.get_barrier_semaphore()
    for where in neighbours:
        pl.semaphore_signal(barrier, inc=1, device_id=where, device_id_type=MESH)

    loads = []

    def load(src, dst):
        copy = pltpu.make_async_copy(src, dst, load_sem.at[len(loads)])
        copy.start()
        loads.append(copy)

    for t in range(2):
        cols = pl.ds(t * LANES, LANES)
        for s in range(SUB):
            rows = pl.ds(ROWS * s, ROWS)
            load(flow_hbm.at[:, rows, cols], raw.at[t, :, :, s, :])
            load(kind_hbm.at[rows, cols], raw_kind.at[t, :, s, :])
    first_natural = len(loads)
    for t in range(2):
        cols = pl.ds(t * LANES, LANES)
        load(flow_hbm.at[:, :, cols], nat.at[t])
        load(kind_hbm.at[:, cols], nat_kind.at[t])
    for copy in loads[:first_natural]:
        copy.wait()

    w_main, w_strip = main_refs[0], strip_refs[0]
    lane = lane_index()

    def part(r, carry):
        lane = lane_index()
        low = lane < LANES // 2
        for c in range(5):
            a, b = (raw_kind[t, r].astype(jnp.float32) if c == 4 else raw[t, c, r] for t in range(2))
            for t in range(2):
                index = jnp.bitwise_and(2 * lane + t, LANES - 1)
                w_main[t, c, r + 2] = jnp.where(low, take(a, index), take(b, index))
        return carry

    loop(0, ROWS, 4, part)
    for copy in loads[first_natural:]:
        copy.wait()

    for side in range(2):
        for i, row in enumerate((0, 248)):
            rows = pl.ds(row, 8)
            total = None
            for c in range(5):
                v = nat_kind[side, rows, :].astype(jnp.float32) if c == 4 else nat[side, c, rows, :]
                if side:
                    v = pltpu.roll(v, -8 * c % LANES, 1)
                    total = v if c == 0 else jnp.where(lane < LANES - 8 * c, v, total)
                else:
                    v = pltpu.roll(v, 8 * c, 1)
                    total = v if c == 0 else jnp.where(lane >= 8 * c, v, total)
            pack[side, i] = total

    for c, source in enumerate((0, 2, 1, 3, 4)):
        for side in range(2):
            for t in range(2):
                rows = pl.ds(t, LANES, stride=2)
                v = nat_kind[side, rows, :].astype(jnp.float32) if c == 4 else nat[side, source, rows, :]
                turned = v.T
                columns[side, t, c] = turned[112:128] if side else turned[0:16]

    refresh_main(w_main)
    pl.semaphore_wait(barrier, 8)
    number = 0
    copies = []

    def send(src, dst, where):
        nonlocal number
        copy = pltpu.make_async_remote_copy(
            src_ref=src, dst_ref=dst, send_sem=send_sem.at[number], recv_sem=recv_sem.at[number],
            device_id=where, device_id_type=MESH)
        copy.start()
        copies.append(copy)
        number += 1

    def strip_at(first, count, sub):
        return w_strip.at[:, :, pl.ds(first, count), sub, :]

    send(w_main.at[:, :, pl.ds(26, 8), 7, :], strip_at(0, 8, TOP), (down, gy))
    send(w_main.at[:, :, pl.ds(2, 8), 0, :], strip_at(16, 8, BOT), (up, gy))
    send(pack.at[1, 1], got.at[0], (down, right))
    send(pack.at[0, 1], got.at[1], (down, left))
    send(pack.at[1, 0], got.at[2], (up, right))
    send(pack.at[0, 0], got.at[3], (up, left))
    top, bottom = w_main.at[:, :, pl.ds(2, 16), 0, :], w_main.at[:, :, pl.ds(18, 16), 7, :]
    send(top, strip_at(8, 16, TOP_L), (gx, right))
    send(top, strip_at(8, 16, TOP_R), (gx, left))
    send(bottom, strip_at(0, 16, BOT_L), (gx, right))
    send(bottom, strip_at(0, 16, BOT_R), (gx, left))
    send(columns.at[1, :, :, pl.ds(8, 8), :], strip_at(0, 8, LEFT), (gx, right))
    send(columns.at[0, :, :, pl.ds(0, 8), :], strip_at(16, 8, RIGHT), (gx, left))

    own = []
    for src, dst in (
        (top, strip_at(8, 16, TOP)),
        (bottom, strip_at(0, 16, BOT)),
        (columns.at[0], strip_at(8, 16, LEFT)),
        (columns.at[1], strip_at(0, 16, RIGHT)),
    ):
        copy = pltpu.make_async_copy(src, dst, copy_sem.at[len(own)])
        copy.start()
        own.append(copy)

    run_to(leg(main_refs, ahead_main, winf_main, MAIN_ROWS, refresh_main, -2), "done")

    for copy in own:
        copy.wait()
    for copy in copies:
        copy.wait_recv()

    def corners(r, carry):
        sub, lane = sub_index(), lane_index()
        total = jnp.zeros((SUB, LANES), jnp.float32)
        for k, where in enumerate((TOP_L, TOP_R, BOT_L, BOT_R)):
            total = jnp.where(sub == where, jnp.broadcast_to(got[k, pl.ds(r, 1), :], (SUB, LANES)), total)
        at_top = jnp.logical_or(sub == TOP_L, sub == TOP_R)
        at_bottom = jnp.logical_or(sub == BOT_L, sub == BOT_R)
        for t in range(2):
            for c in range(5):
                from_left = 120 - 8 * c + 2 * (lane - 124) + t
                from_right = 8 * c + 2 * lane + t
                index = jnp.where(lane >= 124, from_left, jnp.where(lane < 4, from_right, 0))
                v = take(total, index)
                w_strip[t, c, r] = jnp.where(at_top, v, w_strip[t, c, r])
                w_strip[t, c, r + 16] = jnp.where(at_bottom, v, w_strip[t, c, r + 16])
        return carry

    loop(0, 8, 4, corners)
    run_to(leg(strip_refs, ahead_strip, winf_strip, STRIP_ROWS, no_refresh, 0), "done")

    sm_main, fr_main, corr_main = main_refs[3], main_refs[4], main_refs[12]
    sm_strip, fr_strip, corr_strip = strip_refs[3], strip_refs[4], strip_refs[12]

    def gather_columns(i, carry):
        for t in range(2):
            for c, target in enumerate((0, 2, 1, 3)):
                v = sm_strip[t, c, i + 8] + corr_strip[0, c, (i + 8) // 2]
                col_in[t, pl.ds(target * 8 + i, 2, stride=64), :] = v[0:2]
                v = fr_strip[t, c, i + 8]
                col_in[t, pl.ds((target + 4) * 8 + i, 2, stride=64), :] = v[0:2]
        return carry

    loop(0, 8, 2, gather_columns)
    for t in range(2):
        col_turned[t] = col_in[t].T

    def finish(edge):
        def body(k, carry):
            lane, sub = lane_index(), sub_index()
            at_side = jnp.logical_or(lane < 4, lane >= 124)
            even = lane % 2 == 0
            half = lane // 2
            for i in range(2):
                r = 2 * k + i
                side = col_turned[i, pl.ds(k, SUB, stride=16), :]
                for a in range(8):
                    out, c = (out_new, a) if a < 4 else (out_res, a - 4)
                    pair = []
                    for t in range(2):
                        if a < 4:
                            v = sm_main[t, c, r + 2] + corr_main[0, c, k + 2]
                        else:
                            v = fr_main[t, c, r + 2]
                        index = 8 * a + t + 2 * jnp.where(lane < 4, lane, jnp.where(lane >= 124, lane - 92, 0))
                        v = jnp.where(at_side, take(side, index), v)
                        if edge is not None:
                            at, where, first, coarse_first = edge
                            j = r + first
                            s = fr_strip[t, c, j] if a >= 4 else sm_strip[t, c, j] + corr_strip[0, c, k + coarse_first]
                            v = jnp.where(sub == at, sub_roll(s, at - where), v)
                        pair.append(v)
                    for tile in range(2):
                        x, y = (take(v, half + 64 * tile) for v in pair)
                        out[tile, c, r] = jnp.where(even, x, y)
            return carry

        return body

    loop(0, 4, 1, finish((0, TOP, 8, 4)))
    loop(4, 12, 1, finish(None))
    loop(12, 16, 1, finish((7, BOT, -16, -8)))
    for copy in copies:
        copy.wait_send()


def put_kernel(new, res, new_hbm, res_hbm, sems):
    copies = []
    for src, dst in ((new, new_hbm), (res, res_hbm)):
        for t in range(2):
            for s in range(SUB):
                copy = pltpu.make_async_copy(
                    src.at[t, :, :, s, :], dst.at[:, pl.ds(ROWS * s, ROWS), pl.ds(t * LANES, LANES)], sems.at[len(copies)])
                copy.start()
                copies.append(copy)
    for copy in copies:
        copy.wait()


def vmem(*shape):
    return pltpu.VMEM(shape, jnp.float32)


def domain(rows, coarse_rows):
    tile = (SUB, LANES)
    return [
        vmem(2, 5, rows, *tile),
        vmem(2, 4, rows, *tile),
        vmem(2, 4, rows, *tile),
        vmem(2, 4, rows, *tile),
        vmem(2, 4, rows, *tile),
        vmem(1, 4, coarse_rows, *tile),
        vmem(1, 4, coarse_rows, *tile),
        vmem(1, 4, coarse_rows, *tile),
        vmem(1, 4, coarse_rows, *tile),
        vmem(1, coarse_rows, *tile),
        vmem(1, 4, coarse_rows, *tile),
        vmem(1, 4, coarse_rows, *tile),
        vmem(1, 4, coarse_rows, *tile),
        vmem(1, 2, coarse_rows, *tile),
    ]


def solution(mesh):
    nx, ny = mesh.shape["gx"], mesh.shape["gy"]

    def local(flow_state, cell_kind):
        hbm = pl.BlockSpec(memory_space=pl.ANY)
        held = pl.BlockSpec(memory_space=pltpu.VMEM)
        block = (2, 4, ROWS, SUB, LANES)
        new, res = pl.pallas_call(
            functools.partial(kernel, nx, ny),
            out_shape=(vmem(*block), vmem(*block)),
            in_specs=[hbm, hbm],
            out_specs=(held, held),
            scratch_shapes=[
                vmem(*block),
                pltpu.VMEM((2, ROWS, SUB, LANES), jnp.int32),
                vmem(2, 4, 256, LANES),
                pltpu.VMEM((2, 256, LANES), jnp.int32),
                vmem(2, 2, 5, 16, LANES),
                vmem(2, 2, 8, LANES),
                vmem(4, 8, LANES),
                vmem(2, LANES, LANES),
                vmem(2, LANES, LANES),
                *domain(36, 20),
                *domain(24, 12),
                pltpu.SemaphoreType.DMA((36,)),
                pltpu.SemaphoreType.DMA((4,)),
                pltpu.SemaphoreType.DMA((12,)),
                pltpu.SemaphoreType.DMA((12,)),
            ],
            compiler_params=pltpu.CompilerParams(
                collective_id=0, has_side_effects=True, vmem_limit_bytes=64_900_000
            ),
        )(flow_state, cell_kind)
        out = jax.ShapeDtypeStruct(flow_state.shape, jnp.float32)
        return pl.pallas_call(
            put_kernel,
            out_shape=(out, out),
            in_specs=[hbm, hbm],
            out_specs=(hbm, hbm),
            scratch_shapes=[pltpu.SemaphoreType.DMA((32,))],
            compiler_params=pltpu.CompilerParams(vmem_limit_bytes=1 << 20),
        )(new, res)

    return jax.shard_map(
        local,
        mesh=mesh,
        in_specs=(P(None, "gx", "gy"), P("gx", "gy")),
        out_specs=(P(None, "gx", "gy"), P(None, "gx", "gy")),
        check_vma=False,
    )
```

time: 46.7 us -> 33.5 us (0.72)
  Pallas kernels: 42.6 us -> 32.7 us
  local copies, waits for them, and re-layouts: 3.35 us -> 0 us
    pallas_call x1 -> x2, Pallas kernels: 42.6 us -> 32.7 us  [the longest x1 31.2 us: local(): pl.pallas_call(functools.partial(kernel, nx, ny), out_shape=(vmem(*block)...]
    unnamed x4 -> x0, local copies, waits for them, and re-layouts: 3.35 us -> none
where the time goes in v2:
time: 33.5 us; the launch traced here: 33.4 us
  Pallas kernels  32.7 us (98%)
  between operations  0.64 us (2%)
    pallas_call x1, Pallas kernels, local(): pl.pallas_call(functools.partial(kernel, nx, ny), out_shape=(vmem(*block)...  31.2 us
    pallas_call x1, Pallas kernels, local(): pl.pallas_call(put_kernel, out_shape=(out, out), in_specs=[hbm, hbm], out...  1.57 us

profile of v2, /device:TPU:0, one launch (start us, length us, event | category | flops | bytes accessed | tf_op | source)
XLA Modules:
  0.0 33.4 jit_solution(10361558528719109052)
XLA Ops:
  0.6 31.2 %shard_map.41 = (f32[2,4,32,8,128]{4,3,2,1,0:T(8,128)S(1)}, f32[2,4,32,8,128]{4,3,2,1,0:T(8,128)S(1)}) custom-call(f32[4,256,256]{2,1,0:T(8,128)} %flow_hbm.1, s32[256,256]{1,0:T(8,128)} %kind_hbm.1), custom_call_target="tpu_custom_call" | custom-call | tf_op jit(solution)/shard_map/pallas_call | solution.py:567
  31.8 1.6 %shard_map.42 = (f32[4,256,256]{2,1,0:T(8,128)}, f32[4,256,256]{2,1,0:T(8,128)}) custom-call(f32[2,4,32,8,128]{4,3,2,1,0:T(8,128)S(1)} %get-tuple-element.4.new, f32[2,4,32,8,128]{4,3,2,1,0:T(8,128)S(1)} %get-tuple-element.5.res), custom_call_target="tpu_custom_call" | custom-call | tf_op jit(solution)/shard_map/pallas_call | solution.py:594

commit v3 on v2

--- a/solution.py
+++ b/solution.py
@@ -17,7 +17,7 @@
 
 LEFT, RIGHT, TOP_L, TOP, TOP_R, BOT_L, BOT, BOT_R = range(8)
 
-FINE_UNROLL = 2
+FINE_UNROLL = 4
 ROW_UNROLL = 8
 COARSE_UNROLL = 4
 
@@ -325,7 +325,7 @@
 
 
 def kernel(nx, ny, flow_hbm, kind_hbm, out_new, out_res, raw, raw_kind, nat, nat_kind, columns, pack, got, col_in,
-           col_turned, *rest):
+           col_turned, whole, *rest):
     main_refs, strip_refs, sems = rest[:14], rest[14:28], rest[28:]
     load_sem, copy_sem, send_sem, recv_sem = sems
     gx, gy = lax.axis_index("gx"), lax.axis_index("gy")
@@ -360,17 +360,17 @@
     w_main, w_strip = main_refs[0], strip_refs[0]
     lane = lane_index()
 
-    def part(r, carry):
-        lane = lane_index()
+    for t in range(2):
         low = lane < LANES // 2
-        for c in range(5):
-            a, b = (raw_kind[t, r].astype(jnp.float32) if c == 4 else raw[t, c, r] for t in range(2))
-            for t in range(2):
-                index = jnp.bitwise_and(2 * lane + t, LANES - 1)
+        index = jnp.bitwise_and(2 * lane + t, LANES - 1)
+
+        def part(r, carry):
+            for c in range(5):
+                a, b = (raw_kind[s, r].astype(jnp.float32) if c == 4 else raw[s, c, r] for s in range(2))
                 w_main[t, c, r + 2] = jnp.where(low, take(a, index), take(b, index))
-        return carry
-
-    loop(0, ROWS, 4, part)
+            return carry
+
+        loop(0, ROWS, 8, part)
     for copy in loads[first_natural:]:
         copy.wait()
 
@@ -380,13 +380,10 @@
             total = None
             for c in range(5):
                 v = nat_kind[side, rows, :].astype(jnp.float32) if c == 4 else nat[side, c, rows, :]
-                if side:
-                    v = pltpu.roll(v, -8 * c % LANES, 1)
-                    total = v if c == 0 else jnp.where(lane < LANES - 8 * c, v, total)
-                else:
-                    v = pltpu.roll(v, 8 * c, 1)
-                    total = v if c == 0 else jnp.where(lane >= 8 * c, v, total)
-            pack[side, i] = total
+                v = pltpu.roll(v, 8 * (c + side), 1)
+                total = v if c == 0 else jnp.where(lane >= 8 * c, v, total)
+            group = lane // 8
+            pack[side, i] = take(total, 8 * (group // 2) + 2 * (lane % 4) + group % 2)
 
     for c, source in enumerate((0, 2, 1, 3, 4)):
         for side in range(2):
@@ -446,7 +443,7 @@
         copy.wait_recv()
 
     def corners(r, carry):
-        sub, lane = sub_index(), lane_index()
+        sub = sub_index()
         total = jnp.zeros((SUB, LANES), jnp.float32)
         for k, where in enumerate((TOP_L, TOP_R, BOT_L, BOT_R)):
             total = jnp.where(sub == where, jnp.broadcast_to(got[k, pl.ds(r, 1), :], (SUB, LANES)), total)
@@ -454,10 +451,7 @@
         at_bottom = jnp.logical_or(sub == BOT_L, sub == BOT_R)
         for t in range(2):
             for c in range(5):
-                from_left = 120 - 8 * c + 2 * (lane - 124) + t
-                from_right = 8 * c + 2 * lane + t
-                index = jnp.where(lane >= 124, from_left, jnp.where(lane < 4, from_right, 0))
-                v = take(total, index)
+                v = pltpu.roll(total, -(8 * (2 * c + t) + 4) % LANES, 1)
                 w_strip[t, c, r] = jnp.where(at_top, v, w_strip[t, c, r])
                 w_strip[t, c, r + 16] = jnp.where(at_bottom, v, w_strip[t, c, r + 16])
         return carry
@@ -468,54 +462,57 @@
     sm_main, fr_main, corr_main = main_refs[3], main_refs[4], main_refs[12]
     sm_strip, fr_strip, corr_strip = strip_refs[3], strip_refs[4], strip_refs[12]
 
-    def gather_columns(i, carry):
+    for i in range(8):
         for t in range(2):
             for c, target in enumerate((0, 2, 1, 3)):
-                v = sm_strip[t, c, i + 8] + corr_strip[0, c, (i + 8) // 2]
-                col_in[t, pl.ds(target * 8 + i, 2, stride=64), :] = v[0:2]
-                v = fr_strip[t, c, i + 8]
-                col_in[t, pl.ds((target + 4) * 8 + i, 2, stride=64), :] = v[0:2]
-        return carry
-
-    loop(0, 8, 2, gather_columns)
+                for a, v in (
+                    (target, sm_strip[t, c, i + 8] + corr_strip[0, c, (i + 8) // 2]),
+                    (target + 4, fr_strip[t, c, i + 8]),
+                ):
+                    row = 8 * (2 * a + i % 2) + i // 2
+                    col_in[t, pl.ds(row + 4, 1), :] = v[LEFT : LEFT + 1]
+                    col_in[t, pl.ds(row, 1), :] = v[RIGHT : RIGHT + 1]
     for t in range(2):
         col_turned[t] = col_in[t].T
 
-    def finish(edge):
+    def collect(edge):
         def body(k, carry):
             lane, sub = lane_index(), sub_index()
             at_side = jnp.logical_or(lane < 4, lane >= 124)
-            even = lane % 2 == 0
-            half = lane // 2
             for i in range(2):
                 r = 2 * k + i
                 side = col_turned[i, pl.ds(k, SUB, stride=16), :]
                 for a in range(8):
-                    out, c = (out_new, a) if a < 4 else (out_res, a - 4)
-                    pair = []
+                    c = a % 4
                     for t in range(2):
-                        if a < 4:
-                            v = sm_main[t, c, r + 2] + corr_main[0, c, k + 2]
-                        else:
-                            v = fr_main[t, c, r + 2]
-                        index = 8 * a + t + 2 * jnp.where(lane < 4, lane, jnp.where(lane >= 124, lane - 92, 0))
-                        v = jnp.where(at_side, take(side, index), v)
+                        v = fr_main[t, c, r + 2] if a >= 4 else sm_main[t, c, r + 2] + corr_main[0, c, k + 2]
+                        v = jnp.where(at_side, pltpu.roll(side, -(8 * (2 * a + t) + 4) % LANES, 1), v)
                         if edge is not None:
                             at, where, first, coarse_first = edge
                             j = r + first
                             s = fr_strip[t, c, j] if a >= 4 else sm_strip[t, c, j] + corr_strip[0, c, k + coarse_first]
                             v = jnp.where(sub == at, sub_roll(s, at - where), v)
-                        pair.append(v)
-                    for tile in range(2):
-                        x, y = (take(v, half + 64 * tile) for v in pair)
-                        out[tile, c, r] = jnp.where(even, x, y)
+                        whole[t, a, r] = v
             return carry
 
         return body
 
-    loop(0, 4, 1, finish((0, TOP, 8, 4)))
-    loop(4, 12, 1, finish(None))
-    loop(12, 16, 1, finish((7, BOT, -16, -8)))
+    loop(0, 4, 2, collect((0, TOP, 8, 4)))
+    loop(4, 12, 2, collect(None))
+    loop(12, 16, 2, collect((7, BOT, -16, -8)))
+
+    for tile in range(2):
+        even = lane % 2 == 0
+        index = lane // 2 + 64 * tile
+
+        def join(r, carry):
+            for a in range(8):
+                out, c = (out_new, a) if a < 4 else (out_res, a - 4)
+                x, y = (take(whole[t, a, r], index) for t in range(2))
+                out[tile, c, r] = jnp.where(even, x, y)
+            return carry
+
+        loop(0, ROWS, 4, join)
     for copy in copies:
         copy.wait_send()
 
@@ -579,6 +576,7 @@
                 vmem(4, 8, LANES),
                 vmem(2, LANES, LANES),
                 vmem(2, LANES, LANES),
+                vmem(2, 8, ROWS, SUB, LANES),
                 *domain(36, 20),
                 *domain(24, 12),
                 pltpu.SemaphoreType.DMA((36,)),

time: 33.5 us -> 26.2 us (0.78)
  Pallas kernels: 32.7 us -> 25.5 us
    pallas_call x1, Pallas kernels: 31.2 us -> 23.9 us  [local(): pl.pallas_call(functools.partial(kernel, nx, ny), out_shape=(vmem(*block)...]
where the time goes in v3:
time: 26.2 us; the launch traced here: 26.1 us
  Pallas kernels  25.5 us (97%)
  between operations  0.64 us (2%)
    pallas_call x1, Pallas kernels, local(): pl.pallas_call(functools.partial(kernel, nx, ny), out_shape=(vmem(*block)...  23.9 us
    pallas_call x1, Pallas kernels, local(): pl.pallas_call(put_kernel, out_shape=(out, out), in_specs=[hbm, hbm], out...  1.57 us

profile of v3, /device:TPU:0, one launch (start us, length us, event | category | flops | bytes accessed | tf_op | source)
XLA Modules:
  0.0 26.1 jit_solution(16690701010446796682)
XLA Ops:
  0.6 23.9 %shard_map.41 = (f32[2,4,32,8,128]{4,3,2,1,0:T(8,128)S(1)}, f32[2,4,32,8,128]{4,3,2,1,0:T(8,128)S(1)}) custom-call(f32[4,256,256]{2,1,0:T(8,128)} %flow_hbm.1, s32[256,256]{1,0:T(8,128)} %kind_hbm.1), custom_call_target="tpu_custom_call" | custom-call | tf_op jit(solution)/shard_map/pallas_call | solution.py:564
  24.5 1.6 %shard_map.42 = (f32[4,256,256]{2,1,0:T(8,128)}, f32[4,256,256]{2,1,0:T(8,128)}) custom-call(f32[2,4,32,8,128]{4,3,2,1,0:T(8,128)S(1)} %get-tuple-element.4.new, f32[2,4,32,8,128]{4,3,2,1,0:T(8,128)S(1)} %get-tuple-element.5.res), custom_call_target="tpu_custom_call" | custom-call | tf_op jit(solution)/shard_map/pallas_call | solution.py:592

commit v4 on v3

--- a/solution.py
+++ b/solution.py
@@ -18,6 +18,8 @@
 LEFT, RIGHT, TOP_L, TOP, TOP_R, BOT_L, BOT, BOT_R = range(8)
 
 FINE_UNROLL = 4
+JOIN_UNROLL = 8
+PART_UNROLL = 16
 ROW_UNROLL = 8
 COARSE_UNROLL = 4
 
@@ -61,6 +63,26 @@
         return carry
 
     return lax.fori_loop(0, count // unroll, run, carry)
+
+
+def staged_loop(lo, hi, unroll, prepare, body):
+    count = hi - lo
+    while count % unroll:
+        unroll -= 1
+    for i in range(unroll):
+        prepare(lo + i)
+
+    def run(step, carry):
+        first = lo + step * unroll
+        for i in range(unroll):
+            prepare(first + unroll + i)
+        for i in range(unroll):
+            body(first + i)
+        return carry
+
+    lax.fori_loop(0, count // unroll - 1, run, 0)
+    for i in range(unroll):
+        body(hi - unroll + i)
 
 
 def primitives(w_ref, p_ref, tiles, lo, hi, unroll=4):
@@ -95,6 +117,33 @@
     return 0.25 * jnp.abs(ends - twice) / (ends + twice)
 
 
+def shifted_fine(w_ref, p_ref, x_ref, ahead):
+    def shifted(r):
+        for c in range(4):
+            x_ref[c, r] = ahead(w_ref[0, c, r], 1)
+        for i, j in enumerate((0, 2, 3)):
+            x_ref[4 + i, r] = ahead(p_ref[0, j, r], 1)
+        for c in range(4):
+            x_ref[7 + c, r] = ahead(w_ref[1, c, r], 1)
+            x_ref[11 + c, r] = ahead(w_ref[1, c, r], -1)
+        x_ref[15, r] = ahead(p_ref[1, 0, r], 1)
+        x_ref[16, r] = ahead(p_ref[1, 0, r], -1)
+
+    return shifted
+
+
+def shifted_coarse(w_ref, p_ref, x_ref, ahead):
+    def shifted(r):
+        for i, k in enumerate((1, 2, -1)):
+            for c in range(4):
+                x_ref[4 * i + c, r] = ahead(w_ref[0, c, r], k)
+            x_ref[12 + i, r] = ahead(p_ref[0, 0, r], k)
+        x_ref[15, r] = ahead(p_ref[0, 2, r], 1)
+        x_ref[16, r] = ahead(p_ref[0, 3, r], 1)
+
+    return shifted
+
+
 def along_rows(w_ref, p_ref, d_ref, tiles, lo, hi, unroll):
     def flux(t, r):
         w = [w_ref[t, c, r] for c in range(4)]
@@ -140,16 +189,14 @@
     return [w[2], w[1] * q, w[2] * q + press, (w[3] + press) * q]
 
 
-def along_lanes_fine(w_ref, p_ref, d_ref, lo, hi, ahead, emit, unroll):
-    def body(r, carry):
+def along_lanes_fine(w_ref, p_ref, d_ref, x_ref, lo, hi, ahead, emit, unroll):
+    def body(r):
         we, wo = ([w_ref[t, c, r] for c in range(4)] for t in range(2))
         (pe, po), (qe, qo) = ([p_ref[t, i, r] for t in range(2)] for i in (0, 2))
         se, so = jnp.abs(qe) + p_ref[0, 3, r], jnp.abs(qo) + p_ref[1, 3, r]
-        pe1, po1, pom = ahead(pe, 1), ahead(po, 1), ahead(po, -1)
-        qe1, se1 = ahead(qe, 1), ahead(se, 1)
-        we1 = [ahead(v, 1) for v in we]
-        wo1 = [ahead(v, 1) for v in wo]
-        wom = [ahead(v, -1) for v in wo]
+        pe1, po1, pom, qe1 = x_ref[4, r], x_ref[15, r], x_ref[16, r], x_ref[5, r]
+        se1 = jnp.abs(qe1) + x_ref[6, r]
+        we1, wo1, wom = ([x_ref[i + c, r] for c in range(4)] for i in (0, 7, 11))
         ne = quarter_sensor(pom, pe, po)
         no = quarter_sensor(pe, po, pe1)
         ne1 = quarter_sensor(po, pe1, po1)
@@ -165,19 +212,19 @@
             out.append([he - ahead(ho, -1) + d_ref[0, c, r], ho - he + d_ref[1, c, r]])
         for t, w in enumerate((we, wo)):
             emit(t, r, w, [out[c][t] for c in range(4)])
-        return carry
-
-    loop(lo, hi, unroll, body)
-
-
-def along_lanes_coarse(w_ref, p_ref, d_ref, lo, hi, ahead, emit, unroll):
-    def body(r, carry):
+
+    staged_loop(lo, hi, unroll, shifted_fine(w_ref, p_ref, x_ref, ahead), body)
+
+
+def along_lanes_coarse(w_ref, p_ref, d_ref, x_ref, lo, hi, ahead, emit, unroll):
+    def body(r):
         w = [w_ref[0, c, r] for c in range(4)]
         press, q = p_ref[0, 0, r], p_ref[0, 2, r]
         spec = jnp.abs(q) + p_ref[0, 3, r]
-        pm, p1, p2 = ahead(press, -1), ahead(press, 1), ahead(press, 2)
-        q1, s1 = ahead(q, 1), ahead(spec, 1)
-        wm, w1, w2 = ([ahead(v, k) for v in w] for k in (-1, 1, 2))
+        p1, p2, pm = (x_ref[12 + i, r] for i in range(3))
+        q1 = x_ref[15, r]
+        s1 = jnp.abs(q1) + x_ref[16, r]
+        w1, w2, wm = ([x_ref[4 * i + c, r] for c in range(4)] for i in range(3))
         ca, cb = face_coefs(quarter_sensor(pm, press, p1), quarter_sensor(press, p1, p2), spec, s1)
         f, f1 = lane_flux(w, press, q), lane_flux(w1, p1, q1)
         out = []
@@ -185,9 +232,8 @@
             h = f[c] + f1[c] - ca * (w1[c] - w[c]) + cb * ((w2[c] - w1[c]) + (w[c] - wm[c]))
             out.append(h - ahead(h, -1) + d_ref[0, c, r])
         emit(0, r, w, out)
-        return carry
-
-    loop(lo, hi, unroll, body)
+
+    staged_loop(lo, hi, unroll, shifted_coarse(w_ref, p_ref, x_ref, ahead), body)
 
 
 def with_source(w, total, both, far, winf, half_h):
@@ -211,7 +257,7 @@
 
 
 def leg(refs, ahead, winf, rows, refresh, offset):
-    w, pr, dx, sm, fr, cs, cpr, cdx, csum, kk, seg, forc, corr, share = refs
+    w, pr, dx, sm, fr, cs, cpr, cdx, csum, kk, seg, forc, corr, share, x = refs
     (p1, s1, p2, s2, c_state, c_seg, c_prim, c_out) = rows
 
     def smooth(t, r, mine, total):
@@ -230,12 +276,12 @@
     primitives(w, pr, 2, *p1)
     along_rows(w, pr, dx, 2, *s1, ROW_UNROLL)
     yield "rows"
-    along_lanes_fine(w, pr, dx, *s1, ahead, smooth, FINE_UNROLL)
+    along_lanes_fine(w, pr, dx, x, *s1, ahead, smooth, FINE_UNROLL)
     refresh(sm)
     yield "smoothed"
     primitives(sm, pr, 2, *p2)
     along_rows(sm, pr, dx, 2, *s2, ROW_UNROLL)
-    along_lanes_fine(sm, pr, dx, *s2, ahead, fine, FINE_UNROLL)
+    along_lanes_fine(sm, pr, dx, x, *s2, ahead, fine, FINE_UNROLL)
     yield "fine"
 
     def four(get, k):
@@ -279,7 +325,7 @@
             forc[0, c, k] = csum[0, c, k] - res[c]
 
     along_rows(cs, cpr, cdx, 1, *c_out, ROW_UNROLL)
-    along_lanes_coarse(cs, cpr, cdx, *c_out, ahead, force, COARSE_UNROLL)
+    along_lanes_coarse(cs, cpr, cdx, x, *c_out, ahead, force, COARSE_UNROLL)
     primitives(seg, cpr, 1, *c_prim)
 
     def final(t, k, mine, total):
@@ -288,7 +334,7 @@
             corr[0, c, k] = -kk[0, k] * (res[c] + forc[0, c, k])
 
     along_rows(seg, cpr, cdx, 1, *c_out, ROW_UNROLL)
-    along_lanes_coarse(seg, cpr, cdx, *c_out, ahead, final, COARSE_UNROLL)
+    along_lanes_coarse(seg, cpr, cdx, x, *c_out, ahead, final, COARSE_UNROLL)
     yield "done"
 
 
@@ -324,10 +370,10 @@
             return
 
 
-def kernel(nx, ny, flow_hbm, kind_hbm, out_new, out_res, raw, raw_kind, nat, nat_kind, columns, pack, got, col_in,
-           col_turned, whole, *rest):
-    main_refs, strip_refs, sems = rest[:14], rest[14:28], rest[28:]
-    load_sem, copy_sem, send_sem, recv_sem = sems
+def kernel(nx, ny, flow_hbm, kind_hbm, out_new, out_res, raw, raw_kind, nat, nat_kind, columns, pack, got, rows_got,
+           columns_got, col_in, col_turned, spread, *rest):
+    main_refs, strip_refs, sems = rest[:15], rest[15:30], rest[30:]
+    load_sem, send_sem, recv_sem = sems
     gx, gy = lax.axis_index("gx"), lax.axis_index("gy")
     up, down = lax.rem(gx + nx - 1, nx), lax.rem(gx + 1, nx)
     left, right = lax.rem(gy + ny - 1, ny), lax.rem(gy + 1, ny)
@@ -345,37 +391,24 @@
 
     for t in range(2):
         cols = pl.ds(t * LANES, LANES)
+        load(flow_hbm.at[:, :, cols], nat.at[t])
+        load(kind_hbm.at[:, cols], nat_kind.at[t])
+    natural = len(loads)
+    for t in range(2):
+        cols = pl.ds(t * LANES, LANES)
         for s in range(SUB):
             rows = pl.ds(ROWS * s, ROWS)
             load(flow_hbm.at[:, rows, cols], raw.at[t, :, :, s, :])
             load(kind_hbm.at[rows, cols], raw_kind.at[t, :, s, :])
-    first_natural = len(loads)
-    for t in range(2):
-        cols = pl.ds(t * LANES, LANES)
-        load(flow_hbm.at[:, :, cols], nat.at[t])
-        load(kind_hbm.at[:, cols], nat_kind.at[t])
-    for copy in loads[:first_natural]:
-        copy.wait()
 
     w_main, w_strip = main_refs[0], strip_refs[0]
     lane = lane_index()
 
-    for t in range(2):
-        low = lane < LANES // 2
-        index = jnp.bitwise_and(2 * lane + t, LANES - 1)
-
-        def part(r, carry):
-            for c in range(5):
-                a, b = (raw_kind[s, r].astype(jnp.float32) if c == 4 else raw[s, c, r] for s in range(2))
-                w_main[t, c, r + 2] = jnp.where(low, take(a, index), take(b, index))
-            return carry
-
-        loop(0, ROWS, 8, part)
-    for copy in loads[first_natural:]:
+    for copy in loads[:natural]:
         copy.wait()
 
     for side in range(2):
-        for i, row in enumerate((0, 248)):
+        for i, row in enumerate((0, 8, 240, 248)):
             rows = pl.ds(row, 8)
             total = None
             for c in range(5):
@@ -383,18 +416,8 @@
                 v = pltpu.roll(v, 8 * (c + side), 1)
                 total = v if c == 0 else jnp.where(lane >= 8 * c, v, total)
             group = lane // 8
-            pack[side, i] = take(total, 8 * (group // 2) + 2 * (lane % 4) + group % 2)
-
-    for c, source in enumerate((0, 2, 1, 3, 4)):
-        for side in range(2):
-            for t in range(2):
-                rows = pl.ds(t, LANES, stride=2)
-                v = nat_kind[side, rows, :].astype(jnp.float32) if c == 4 else nat[side, source, rows, :]
-                turned = v.T
-                columns[side, t, c] = turned[112:128] if side else turned[0:16]
-
-    refresh_main(w_main)
-    pl.semaphore_wait(barrier, 8)
+            pack[side, pl.ds(8 * i, 8), :] = take(total, 8 * (group // 2) + 2 * (lane % 4) + group % 2)
+
     number = 0
     copies = []
 
@@ -407,60 +430,124 @@
         copies.append(copy)
         number += 1
 
-    def strip_at(first, count, sub):
-        return w_strip.at[:, :, pl.ds(first, count), sub, :]
-
-    send(w_main.at[:, :, pl.ds(26, 8), 7, :], strip_at(0, 8, TOP), (down, gy))
-    send(w_main.at[:, :, pl.ds(2, 8), 0, :], strip_at(16, 8, BOT), (up, gy))
-    send(pack.at[1, 1], got.at[0], (down, right))
-    send(pack.at[0, 1], got.at[1], (down, left))
-    send(pack.at[1, 0], got.at[2], (up, right))
-    send(pack.at[0, 0], got.at[3], (up, left))
-    top, bottom = w_main.at[:, :, pl.ds(2, 16), 0, :], w_main.at[:, :, pl.ds(18, 16), 7, :]
-    send(top, strip_at(8, 16, TOP_L), (gx, right))
-    send(top, strip_at(8, 16, TOP_R), (gx, left))
-    send(bottom, strip_at(0, 16, BOT_L), (gx, right))
-    send(bottom, strip_at(0, 16, BOT_R), (gx, left))
-    send(columns.at[1, :, :, pl.ds(8, 8), :], strip_at(0, 8, LEFT), (gx, right))
-    send(columns.at[0, :, :, pl.ds(0, 8), :], strip_at(16, 8, RIGHT), (gx, left))
-
-    own = []
-    for src, dst in (
-        (top, strip_at(8, 16, TOP)),
-        (bottom, strip_at(0, 16, BOT)),
-        (columns.at[0], strip_at(8, 16, LEFT)),
-        (columns.at[1], strip_at(0, 16, RIGHT)),
-    ):
-        copy = pltpu.make_async_copy(src, dst, copy_sem.at[len(own)])
-        copy.start()
-        own.append(copy)
-
-    run_to(leg(main_refs, ahead_main, winf_main, MAIN_ROWS, refresh_main, -2), "done")
-
-    for copy in own:
+    for copy in loads[natural:]:
         copy.wait()
+
+    for t in range(2):
+        low = lane < LANES // 2
+        index = jnp.bitwise_and(2 * lane + t, LANES - 1)
+
+        def part(r, carry):
+            for c in range(5):
+                a, b = (raw_kind[s, r].astype(jnp.float32) if c == 4 else raw[s, c, r] for s in range(2))
+                w_main[t, c, r + 2] = jnp.where(low, take(a, index), take(b, index))
+            return carry
+
+        loop(0, ROWS, PART_UNROLL, part)
+
+    for c, source in enumerate((0, 2, 1, 3, 4)):
+        for side in range(2):
+            for t in range(2):
+                rows = pl.ds(t, LANES, stride=2)
+                v = nat_kind[side, rows, :].astype(jnp.float32) if c == 4 else nat[side, source, rows, :]
+                turned = v.T
+                columns[side, t, c] = turned[112:128] if side else turned[0:16]
+
+    column = lax.broadcasted_iota(jnp.int32, (2 * LANES, 2 * LANES), 1)
+    source = lax.broadcasted_iota(jnp.int32, (2 * LANES, 2 * LANES), 0)
+    ones = jnp.where(column == 2 * (source % LANES) + source // LANES, 1.0, 0.0).astype(jnp.bfloat16)
+    for i in range(3):
+        spread[pl.ds(2 * LANES * i, 2 * LANES), :] = ones
+
+    def own(base):
+        def body(i, carry):
+            sub = sub_index()
+            r = i + base
+            for t in range(2):
+                for c in range(5):
+                    v = jnp.zeros((SUB, LANES), jnp.float32)
+                    if base >= 8:
+                        v = jnp.where(sub == TOP, sub_roll(w_main[t, c, r - 6], TOP), v)
+                        v = jnp.where(sub == LEFT, jnp.broadcast_to(columns[0, t, c, pl.ds(r - 8, 1), :], (SUB, LANES)), v)
+                    if base <= 8:
+                        v = jnp.where(sub == BOT, sub_roll(w_main[t, c, r + 18], BOT - 7), v)
+                        v = jnp.where(sub == RIGHT, jnp.broadcast_to(columns[1, t, c, pl.ds(r, 1), :], (SUB, LANES)), v)
+                    w_strip[t, c, r] = v
+            return carry
+
+        loop(0, 8, 4, body)
+
+    def arrived(base):
+        def body(i, carry):
+            sub = sub_index()
+            r = i + base
+            total = jnp.zeros((SUB, LANES), jnp.float32)
+            for where, side, row in ((TOP_L, 0, r), (TOP_R, 1, r), (BOT_L, 0, r + 24), (BOT_R, 1, r + 24)):
+                total = jnp.where(sub == where, jnp.broadcast_to(got[side, pl.ds(row, 1), :], (SUB, LANES)), total)
+            at_halo = jnp.logical_and(sub >= TOP_L, jnp.logical_and(sub != TOP, sub != BOT))
+            for t in range(2):
+                for c in range(5):
+                    v = jnp.where(at_halo, pltpu.roll(total, -(8 * (2 * c + t) + 4) % LANES, 1), w_strip[t, c, r])
+                    for k, first, at_row, at_column in ((0, 0, TOP, LEFT), (1, 16, BOT, RIGHT)):
+                        if base == first:
+                            v = jnp.where(sub == at_row, jnp.broadcast_to(rows_got[k, t, c, pl.ds(i, 1), :], (SUB, LANES)), v)
+                            v = jnp.where(
+                                sub == at_column, jnp.broadcast_to(columns_got[k, t, c, pl.ds(i, 1), :], (SUB, LANES)), v)
+                    w_strip[t, c, r] = v
+            return carry
+
+        loop(0, 8, 4, body)
+
+    refresh_main(w_main)
+    main = leg(main_refs, ahead_main, winf_main, MAIN_ROWS, refresh_main, -2)
+    run_to(main, "smoothed")
+    pl.semaphore_wait(barrier, 8)
+    send(pack.at[1, pl.ds(24, 8)], got.at[0, pl.ds(0, 8)], (down, right))
+    send(pack.at[0, pl.ds(24, 8)], got.at[1, pl.ds(0, 8)], (down, left))
+    send(pack.at[1, pl.ds(0, 8)], got.at[0, pl.ds(40, 8)], (up, right))
+    send(pack.at[0, pl.ds(0, 8)], got.at[1, pl.ds(40, 8)], (up, left))
+    send(w_main.at[:, :, pl.ds(26, 8), 7, :], rows_got.at[0], (down, gy))
+    send(w_main.at[:, :, pl.ds(2, 8), 0, :], rows_got.at[1], (up, gy))
+    send(pack.at[1], got.at[0, pl.ds(8, 32)], (gx, right))
+    send(pack.at[0], got.at[1, pl.ds(8, 32)], (gx, left))
+    send(columns.at[1, :, :, pl.ds(8, 8), :], columns_got.at[0], (gx, right))
+    send(columns.at[0, :, :, pl.ds(0, 8), :], columns_got.at[1], (gx, left))
+    for base in (0, 8, 16):
+        own(base)
+    run_to(main, "done")
+
+    sm_main, fr_main, corr_main = main_refs[3], main_refs[4], main_refs[12]
+    sm_strip, fr_strip, corr_strip = strip_refs[3], strip_refs[4], strip_refs[12]
+
+    def in_order(even, odd):
+        x = jnp.concatenate([jnp.concatenate(even, 0), jnp.concatenate(odd, 0)], 1)
+        high = x.astype(jnp.bfloat16)
+        rest = x - high.astype(jnp.float32)
+        middle = rest.astype(jnp.bfloat16)
+        low = (rest - middle.astype(jnp.float32)).astype(jnp.bfloat16)
+        return jnp.dot(jnp.concatenate([high, middle, low], 1), spread[...], preferred_element_type=jnp.float32)
+
+    def join_main(c, carry):
+        for out in (out_new, out_res):
+            for half in range(2):
+                span = range(16 * half, 16 * half + 16)
+                if out is out_new:
+                    tiles = [[sm_main[t, c, r + 2] + corr_main[0, c, r // 2 + 2] for r in span] for t in range(2)]
+                else:
+                    tiles = [[fr_main[t, c, r + 2] for r in span] for t in range(2)]
+                y = in_order(*tiles)
+                for tile in range(2):
+                    for i, r in enumerate(span):
+                        out[tile, c, r] = y[8 * i : 8 * i + 8, LANES * tile : LANES * tile + LANES]
+        return carry
+
+    lax.fori_loop(0, 4, join_main, 0)
+
     for copy in copies:
         copy.wait_recv()
-
-    def corners(r, carry):
-        sub = sub_index()
-        total = jnp.zeros((SUB, LANES), jnp.float32)
-        for k, where in enumerate((TOP_L, TOP_R, BOT_L, BOT_R)):
-            total = jnp.where(sub == where, jnp.broadcast_to(got[k, pl.ds(r, 1), :], (SUB, LANES)), total)
-        at_top = jnp.logical_or(sub == TOP_L, sub == TOP_R)
-        at_bottom = jnp.logical_or(sub == BOT_L, sub == BOT_R)
-        for t in range(2):
-            for c in range(5):
-                v = pltpu.roll(total, -(8 * (2 * c + t) + 4) % LANES, 1)
-                w_strip[t, c, r] = jnp.where(at_top, v, w_strip[t, c, r])
-                w_strip[t, c, r + 16] = jnp.where(at_bottom, v, w_strip[t, c, r + 16])
-        return carry
-
-    loop(0, 8, 4, corners)
+    for base in (0, 8, 16):
+        arrived(base)
     run_to(leg(strip_refs, ahead_strip, winf_strip, STRIP_ROWS, no_refresh, 0), "done")
-
-    sm_main, fr_main, corr_main = main_refs[3], main_refs[4], main_refs[12]
-    sm_strip, fr_strip, corr_strip = strip_refs[3], strip_refs[4], strip_refs[12]
 
     for i in range(8):
         for t in range(2):
@@ -469,50 +556,41 @@
                     (target, sm_strip[t, c, i + 8] + corr_strip[0, c, (i + 8) // 2]),
                     (target + 4, fr_strip[t, c, i + 8]),
                 ):
-                    row = 8 * (2 * a + i % 2) + i // 2
-                    col_in[t, pl.ds(row + 4, 1), :] = v[LEFT : LEFT + 1]
-                    col_in[t, pl.ds(row, 1), :] = v[RIGHT : RIGHT + 1]
+                    col_in[t, pl.ds(16 * a + 8 + i, 1), :] = v[LEFT : LEFT + 1]
+                    col_in[t, pl.ds(16 * a + i, 1), :] = v[RIGHT : RIGHT + 1]
     for t in range(2):
         col_turned[t] = col_in[t].T
 
-    def collect(edge):
-        def body(k, carry):
-            lane, sub = lane_index(), sub_index()
-            at_side = jnp.logical_or(lane < 4, lane >= 124)
-            for i in range(2):
-                r = 2 * k + i
-                side = col_turned[i, pl.ds(k, SUB, stride=16), :]
-                for a in range(8):
-                    c = a % 4
-                    for t in range(2):
-                        v = fr_main[t, c, r + 2] if a >= 4 else sm_main[t, c, r + 2] + corr_main[0, c, k + 2]
-                        v = jnp.where(at_side, pltpu.roll(side, -(8 * (2 * a + t) + 4) % LANES, 1), v)
-                        if edge is not None:
-                            at, where, first, coarse_first = edge
-                            j = r + first
-                            s = fr_strip[t, c, j] if a >= 4 else sm_strip[t, c, j] + corr_strip[0, c, k + coarse_first]
-                            v = jnp.where(sub == at, sub_roll(s, at - where), v)
-                        whole[t, a, r] = v
-            return carry
-
-        return body
-
-    loop(0, 4, 2, collect((0, TOP, 8, 4)))
-    loop(4, 12, 2, collect(None))
-    loop(12, 16, 2, collect((7, BOT, -16, -8)))
-
-    for tile in range(2):
-        even = lane % 2 == 0
-        index = lane // 2 + 64 * tile
-
-        def join(r, carry):
+    def sides(k, carry):
+        lane = lane_index()
+        for i in range(2):
+            side = col_turned[i, pl.ds(k, SUB, stride=16), :]
+            r = 2 * k + i
             for a in range(8):
                 out, c = (out_new, a) if a < 4 else (out_res, a - 4)
-                x, y = (take(whole[t, a, r], index) for t in range(2))
-                out[tile, c, r] = jnp.where(even, x, y)
-            return carry
-
-        loop(0, ROWS, 4, join)
+                v = pltpu.roll(side, -(16 * a + 8) % LANES, 1)
+                out[0, c, r] = jnp.where(lane < 8, v, out[0, c, r])
+                out[1, c, r] = jnp.where(lane >= LANES - 8, v, out[1, c, r])
+        return carry
+
+    loop(0, 16, 4, sides)
+
+    def ends(c, carry):
+        sub = sub_index()
+        for out in (out_new, out_res):
+            if out is out_new:
+                tiles = [[sm_strip[t, c, r] + corr_strip[0, c, r // 2] for r in range(8, 16)] for t in range(2)]
+            else:
+                tiles = [[fr_strip[t, c, r] for r in range(8, 16)] for t in range(2)]
+            y = in_order(*tiles)
+            for tile in range(2):
+                for r in range(8):
+                    v = y[8 * r : 8 * r + 8, LANES * tile : LANES * tile + LANES]
+                    out[tile, c, r] = jnp.where(sub == 0, sub_roll(v, -TOP), out[tile, c, r])
+                    out[tile, c, r + 24] = jnp.where(sub == 7, sub_roll(v, 7 - BOT), out[tile, c, r + 24])
+        return carry
+
+    lax.fori_loop(0, 4, ends, 0)
     for copy in copies:
         copy.wait_send()
 
@@ -551,6 +629,7 @@
         vmem(1, 4, coarse_rows, *tile),
         vmem(1, 4, coarse_rows, *tile),
         vmem(1, 2, coarse_rows, *tile),
+        vmem(17, rows, *tile),
     ]
 
 
@@ -572,17 +651,18 @@
                 vmem(2, 4, 256, LANES),
                 pltpu.VMEM((2, 256, LANES), jnp.int32),
                 vmem(2, 2, 5, 16, LANES),
-                vmem(2, 2, 8, LANES),
-                vmem(4, 8, LANES),
+                vmem(2, 32, LANES),
+                vmem(2, 48, LANES),
+                vmem(2, 2, 5, 8, LANES),
+                vmem(2, 2, 5, 8, LANES),
                 vmem(2, LANES, LANES),
                 vmem(2, LANES, LANES),
-                vmem(2, 8, ROWS, SUB, LANES),
+                pltpu.VMEM((6 * LANES, 2 * LANES), jnp.bfloat16),
                 *domain(36, 20),
                 *domain(24, 12),
                 pltpu.SemaphoreType.DMA((36,)),
-                pltpu.SemaphoreType.DMA((4,)),
-                pltpu.SemaphoreType.DMA((12,)),
-                pltpu.SemaphoreType.DMA((12,)),
+                pltpu.SemaphoreType.DMA((10,)),
+                pltpu.SemaphoreType.DMA((10,)),
             ],
             compiler_params=pltpu.CompilerParams(
                 collective_id=0, has_side_effects=True, vmem_limit_bytes=64_900_000

time: 26.2 us -> 23.8 us (0.908)
  Pallas kernels: 25.5 us -> 23 us
    pallas_call x1, Pallas kernels: 23.9 us -> 21.4 us  [local(): pl.pallas_call(functools.partial(kernel, nx, ny), out_shape=(vmem(*block)...]
where the time goes in v4:
time: 23.8 us; the launch traced here: 23.6 us
  Pallas kernels  23 us (97%)
  between operations  0.64 us (3%)
    pallas_call x1, Pallas kernels, local(): pl.pallas_call(functools.partial(kernel, nx, ny), out_shape=(vmem(*block)...  21.4 us
    pallas_call x1, Pallas kernels, local(): pl.pallas_call(put_kernel, out_shape=(out, out), in_specs=[hbm, hbm], out...  1.57 us

profile of v4, /device:TPU:0, one launch (start us, length us, event | category | flops | bytes accessed | tf_op | source)
XLA Modules:
  0.0 23.6 jit_solution(2710425241799368276)
XLA Ops:
  0.6 21.4 %shard_map.41 = (f32[2,4,32,8,128]{4,3,2,1,0:T(8,128)S(1)}, f32[2,4,32,8,128]{4,3,2,1,0:T(8,128)S(1)}) custom-call(f32[4,256,256]{2,1,0:T(8,128)} %flow_hbm.1, s32[256,256]{1,0:T(8,128)} %kind_hbm.1), custom_call_target="tpu_custom_call" | custom-call | tf_op jit(solution)/shard_map/pallas_call | solution.py:643
  22.0 1.6 %shard_map.42 = (f32[4,256,256]{2,1,0:T(8,128)}, f32[4,256,256]{2,1,0:T(8,128)}) custom-call(f32[2,4,32,8,128]{4,3,2,1,0:T(8,128)S(1)} %get-tuple-element.4.new, f32[2,4,32,8,128]{4,3,2,1,0:T(8,128)S(1)} %get-tuple-element.5.res), custom_call_target="tpu_custom_call" | custom-call | tf_op jit(solution)/shard_map/pallas_call | solution.py:672

commit v5 on v4

--- a/solution.py
+++ b/solution.py
@@ -496,7 +496,7 @@
                     w_strip[t, c, r] = v
             return carry
 
-        loop(0, 8, 4, body)
+        loop(0, 8, 8, body)
 
     refresh_main(w_main)
     main = leg(main_refs, ahead_main, winf_main, MAIN_ROWS, refresh_main, -2)
@@ -541,7 +541,8 @@
                         out[tile, c, r] = y[8 * i : 8 * i + 8, LANES * tile : LANES * tile + LANES]
         return carry
 
-    lax.fori_loop(0, 4, join_main, 0)
+    for c in range(4):
+        join_main(c, 0)
 
     for copy in copies:
         copy.wait_recv()
@@ -590,7 +591,8 @@
                     out[tile, c, r + 24] = jnp.where(sub == 7, sub_roll(v, 7 - BOT), out[tile, c, r + 24])
         return carry
 
-    lax.fori_loop(0, 4, ends, 0)
+    for c in range(4):
+        ends(c, 0)
     for copy in copies:
         copy.wait_send()
 

time: 23.8 us -> 23 us (0.966)
  Pallas kernels: 23 us -> 22.2 us
    pallas_call x1, Pallas kernels: 21.4 us -> 20.7 us  [local(): pl.pallas_call(functools.partial(kernel, nx, ny), out_shape=(vmem(*block)...]
where the time goes in v5:
time: 23 us; the launch traced here: 22.9 us
  Pallas kernels  22.2 us (97%)
  between operations  0.64 us (3%)
    pallas_call x1, Pallas kernels, local(): pl.pallas_call(functools.partial(kernel, nx, ny), out_shape=(vmem(*block)...  20.7 us
    pallas_call x1, Pallas kernels, local(): pl.pallas_call(put_kernel, out_shape=(out, out), in_specs=[hbm, hbm], out...  1.57 us

profile of v5, /device:TPU:0, one launch (start us, length us, event | category | flops | bytes accessed | tf_op | source)
XLA Modules:
  0.0 22.9 jit_solution(870756089428226976)
XLA Ops:
  0.6 20.7 %shard_map.41 = (f32[2,4,32,8,128]{4,3,2,1,0:T(8,128)S(1)}, f32[2,4,32,8,128]{4,3,2,1,0:T(8,128)S(1)}) custom-call(f32[4,256,256]{2,1,0:T(8,128)} %flow_hbm.1, s32[256,256]{1,0:T(8,128)} %kind_hbm.1), custom_call_target="tpu_custom_call" | custom-call | tf_op jit(solution)/shard_map/pallas_call | solution.py:645
  21.3 1.6 %shard_map.42 = (f32[4,256,256]{2,1,0:T(8,128)}, f32[4,256,256]{2,1,0:T(8,128)}) custom-call(f32[2,4,32,8,128]{4,3,2,1,0:T(8,128)S(1)} %get-tuple-element.4.new, f32[2,4,32,8,128]{4,3,2,1,0:T(8,128)S(1)} %get-tuple-element.5.res), custom_call_target="tpu_custom_call" | custom-call | tf_op jit(solution)/shard_map/pallas_call | solution.py:674
